TPU v7x, 32 devices: a whole 2x2x4 slice. The times are simulated.
32 devices in a mesh: ga: 2 (over y), gx: 16 (over z, x, core).
Axes of the slice: x: 2, y: 2, z: 4, core: 2. Of those that a mesh axis runs over, the one named last changes fastest.
Arguments:
- fields: bfloat16 [2048, 512, 128], P('gx', 'ga'), parts along dimension 1, may hold values from -6 to 6
- cotangent: bfloat16 [2048, 512, 128], P('gx', 'ga'), parts along dimension 1, may hold values from -6 to 6
- point_weight: bfloat16 [128, 128], replicated, may hold values from -0.5 to 0.5
- mix_weight: bfloat16 [12, 128, 128], replicated, may hold values from -0.5 to 0.5
- bias_vec: bfloat16 [128], replicated, may hold values from -3 to 3
Outputs:
- grad_input: bfloat16 [2048, 512, 128], P('gx', 'ga'), parts along dimension 1
- grad_mix: bfloat16 [24, 128, 128], P('ga'), parts along dimension 0
- grad_point: bfloat16 [256, 128], P('ga'), parts along dimension 0
- grad_bias: bfloat16 [256], P('ga'), parts along dimension 0
There are 2 independent parts, one for each index of `ga`. A program takes and returns all parts, laid end to end along the dimension named above; an argument that names none is the same for every part. Nothing has to cross between parts.
All inputs are finite; a program needn't handle non-finite values.
Results may differ from a plain program's by a relative error of at most 0.012.
Values sent between devices are 32-bit elements; how exact they have to be, the bound alone decides.
A program may use at most 128 MiB of HBM per device.

v0:
```python
import math

import jax
import jax.numpy as jnp
import numpy as np
from jax import lax
from jax.sharding import PartitionSpec as P

NX = 2048
LEVELS = 11


root_half = 0.7071067811865476


def partner_2(block, axis, stride):
    count = lax.axis_size(axis)
    route = []
    for low in range(count):
        high = low | 1 << stride
        if high != low and high < count:
            route += [(low, high), (high, low)]
    return lax.ppermute(block, axis, route)


def haar_forward(signal, depth_count):
    for degree in range(depth_count):
        stride = 2**degree
        shaped = signal.reshape((signal.shape[0] // (2 * stride), 2, stride) + signal.shape[1:])
        even_rows = shaped[:, 0, 0]
        odd_rows = shaped[:, 1, 0]
        shaped = shaped.at[:, 0, 0].set((even_rows + odd_rows) * root_half)
        shaped = shaped.at[:, 1, 0].set((odd_rows - even_rows) * root_half)
        signal = shaped.reshape(signal.shape)
    return signal


def haar_inverse(signal, depth_count):
    for degree in reversed(range(depth_count)):
        stride = 2**degree
        shaped = signal.reshape((signal.shape[0] // (2 * stride), 2, stride) + signal.shape[1:])
        coarse_rows = shaped[:, 0, 0]
        detail_rows = shaped[:, 1, 0]
        shaped = shaped.at[:, 0, 0].set((coarse_rows - detail_rows) * root_half)
        shaped = shaped.at[:, 1, 0].set((coarse_rows + detail_rows) * root_half)
        signal = shaped.reshape(signal.shape)
    return signal


def mix_levels(coeffs_b, weights, depth_count, first_weight):
    output = jnp.zeros(coeffs_b.shape, jnp.float32)
    for degree in range(depth_count):
        stride = 2**degree
        picked = coeffs_b[stride :: 2 * stride]
        output = output.at[stride :: 2 * stride].set(
            jnp.dot(picked, weights[degree], preferred_element_type=jnp.float32)
        )
    output = output.at[0].set(
        jnp.dot(coeffs_b[0], first_weight, preferred_element_type=jnp.float32)
    )
    return output


def outer_sum(left, right):
    left_flat = left.reshape((-1, left.shape[-1]))
    right_flat = right.reshape((-1, right.shape[-1]))
    return lax.dot_general(
        left_flat, right_flat, (((0,), (0,)), ((), ())), preferred_element_type=jnp.float32
    )


def gelu_slope(pre_act, cotangent):
    unused_out, pullback = jax.vjp(jax.nn.gelu, pre_act)
    return pullback(cotangent.astype(pre_act.dtype))[0].astype(jnp.bfloat16)


def level_factors(columns):
    counts = [columns * NX / 2 ** (degree + 1) for degree in range(LEVELS)] + [columns]
    return np.array([1.0 / math.sqrt(value) for value in counts], np.float32)


def cross_levels(carry_row, inverse, position, cross_depth):
    degrees = list(range(cross_depth))
    if inverse:
        degrees = degrees[::-1]
    for degree in degrees:
        partner = partner_2(carry_row, "gx", degree)
        upper_half = position // 2**degree % 2 == 1
        active = position % 2**degree == 0
        summed = (carry_row + partner) * root_half
        differ = (carry_row - partner) * root_half
        if inverse:
            moved_row = jnp.where(upper_half, summed, differ)
        else:
            moved_row = jnp.where(upper_half, differ, summed)
        carry_row = jnp.where(active, moved_row, carry_row)
    return carry_row


def transform(signal, inverse, local_depth, position, cross_depth):
    if inverse:
        signal = signal.at[0].set(cross_levels(signal[0], True, position, cross_depth))
        return haar_inverse(signal, local_depth)
    signal = haar_forward(signal, local_depth)
    return signal.at[0].set(cross_levels(signal[0], False, position, cross_depth))


def shards(fields, cotangent, point_weight, mix_weight, bias_vec):
    rows_local = fields.shape[0]
    local_depth = rows_local.bit_length() - 1
    device_count = lax.axis_size("gx")
    cross_depth = device_count.bit_length() - 1
    position = lax.axis_index("gx")
    trailing = jnp.zeros((), jnp.int32)
    for degree in range(cross_depth):
        trailing = trailing + (position % 2 ** (degree + 1) == 0).astype(jnp.int32)
    first_level = local_depth + trailing
    transposed = jnp.swapaxes(mix_weight, 1, 2)
    first_weight = lax.dynamic_index_in_dim(mix_weight, first_level, 0, keepdims=False)
    first_back = lax.dynamic_index_in_dim(transposed, first_level, 0, keepdims=False)
    empty_grad = jnp.zeros((mix_weight.shape[1], mix_weight.shape[2]), jnp.float32)
    coeffs = transform(fields.astype(jnp.float32), False, local_depth, position, cross_depth)
    coeffs_b = coeffs.astype(jnp.bfloat16)
    mixed_rows = mix_levels(coeffs_b, mix_weight, local_depth, first_weight)
    spectral = transform(mixed_rows, True, local_depth, position, cross_depth)
    pre_act = (
        spectral
        + jnp.dot(fields, point_weight, preferred_element_type=jnp.float32)
        + bias_vec.astype(jnp.float32)
    )
    slope_b = gelu_slope(pre_act, cotangent)
    back_coeffs = transform(slope_b.astype(jnp.float32), False, local_depth, position, cross_depth)
    back_b = back_coeffs.astype(jnp.bfloat16)
    grads_list = []
    for degree in range(local_depth):
        stride = 2**degree
        grads_list.append(outer_sum(coeffs_b[stride :: 2 * stride], back_b[stride :: 2 * stride]))
    grads_list = grads_list + [empty_grad] * (LEVELS + 1 - local_depth)
    onehot = (jnp.arange(LEVELS + 1, dtype=jnp.int32) == first_level).astype(jnp.float32)
    stacked = (
        jnp.stack(grads_list) + onehot[:, None, None] * outer_sum(coeffs_b[0:1], back_b[0:1])[None]
    )
    point_grad = outer_sum(fields, slope_b)
    bias_grad = jnp.sum(slope_b.astype(jnp.float32), axis=(0, 1))
    back_mixed = mix_levels(back_b, transposed, local_depth, first_back)
    spectral_back = transform(back_mixed, True, local_depth, position, cross_depth)
    totals = lax.psum((stacked, point_grad, bias_grad), "gx")
    factors = jnp.asarray(level_factors(fields.shape[1]))
    scale_all = 1.0 / math.sqrt(NX * fields.shape[1])
    grad_mix = (totals[0] * factors[:, None, None]).astype(jnp.bfloat16)
    grad_point = (totals[1] * scale_all).astype(jnp.bfloat16)
    grad_bias = (totals[2] * scale_all).astype(jnp.bfloat16)
    grad_input = (
        spectral_back + jnp.dot(slope_b, point_weight.T, preferred_element_type=jnp.float32)
    ).astype(jnp.bfloat16)
    return (grad_input, grad_mix, grad_point, grad_bias)


def solution(mesh):
    in_specs = (P("gx", "ga", None), P("gx", "ga", None), P(), P(), P())
    out_specs = (P("gx", "ga", None), P("ga", None, None), P("ga", None), P("ga"))
    return jax.shard_map(shards, mesh=mesh, in_specs=in_specs, out_specs=out_specs, check_vma=False)
```

profile of v0, /device:TPU:0, one launch (start us, length us, event | category | flops | bytes accessed | tf_op | source)
XLA Modules:
  0.0 672.7 jit_solution(4957681307654745231)
XLA Ops:
  7.2 11.5 %convert.1 = f32[64,2,1,256,128]{4,3,1,0,2:T(8,128)} convert(bf16[64,2,1,256,128]{4,3,1,0,2:T(8,128)(2,1)} %bitcast.252) | non-fusion elementwise | flops 4194304 | bytes 25165824 | tf_op jit(solution)/shard_map/reshape | solution.py:29
  18.8 5.8 copy-done.3
  27.6 6.9 %multiply_dynamic-update-slice_fusion.6 = f32[64,2,1,256,128]{4,3,1,0,2:T(8,128)S(1)} fusion(f32[64,2,1,256,128]{4,3,1,0,2:T(8,128)S(1)} %multiply_dynamic-update-slice_fusion.7, f32[64,2,1,256,128]{4,3,1,0,2:T(8,128)} %convert.1), kind=kLoop, calls=%fused_computation.36 | loop fusion | flops 4194304 | bytes 25165824 | tf_op jit(solution)/shard_map/scatter | solution.py:33
  48.0 5.8 copy.30
  96.1 6.6 convert_element_type.52
  102.7 6.1 fusion.17
  117.2 7.8 %broadcast.1003.clone = f32[128,256,128]{2,1,0:T(8,128)} broadcast(f32[]{:T(128)} %constant.1621.clone.1), dimensions={} | broadcast | bytes 16777220 | tf_op jit(solution)/shard_map/broadcast.42
  125.1 16.3 %scatter_fusion = f32[128,256,128]{2,1,0:T(8,128)} fusion(f32[128,256,128]{2,1,0:T(8,128)} %broadcast.1003.clone, s32[64]{0:T(128)S(1)} %add_bitcast_fusion.5, f32[64,256,128]{2,1,0:T(8,128)} %fusion.17), kind=kCustom, calls=%fused_computation | custom fusion | bytes 25166080 | tf_op jit(solution)/shard_map/scatter | solution.py:55
  141.4 8.3 %scatter_fusion.1 = f32[128,256,128]{2,1,0:T(8,128)} fusion(f32[128,256,128]{2,1,0:T(8,128)} %scatter_fusion, s32[32]{0:T(128)S(1)} %add_bitcast_fusion.4, f32[32,256,128]{2,1,0:T(8,128)} %fusion.24), kind=kCustom, calls=%fused_computation.1 | custom fusion | bytes 12583040 | tf_op jit(solution)/shard_map/scatter | solution.py:55
  165.6 6.5 collective-permute-done.4
  184.3 5.8 copy.50
  213.8 5.8 copy.62
  228.5 11.6 %multiply_dynamic-update-slice_fusion.5 = f32[64,2,1,256,128]{4,3,1,0,2:T(8,128)} fusion(f32[64,2,1,256,128]{4,3,1,0,2:T(8,128)} %copy.62, f32[64,1,1,256,128]{4,3,1,0,2:T(8,128)} %slice.2362), kind=kLoop, calls=%fused_computation.35 | loop fusion | flops 4194304 | bytes 25165824 | tf_op jit(solution)/shard_map/scatter | solution.py:44
  240.1 10.3 %multiply_dynamic-update-slice_fusion.4 = f32[64,2,1,256,128]{4,3,1,0,2:T(8,128)} fusion(f32[64,2,1,256,128]{4,3,1,0,2:T(8,128)} %multiply_dynamic-update-slice_fusion.5, f32[64,2,1,256,128]{4,3,1,0,2:T(8,128)} %bitcast.220), kind=kLoop, calls=%fused_computation.34 | loop fusion | flops 4194304 | bytes 25165824 | tf_op jit(solution)/shard_map/scatter | solution.py:45
  250.4 28.9 %convert_reduce_fusion = (f32[128]{0:T(128)S(1)}, bf16[128,256,128]{2,1,0:T(8,128)(2,1)}) fusion(f32[128]{0:T(128)S(1)} %convert_element_type.57, bf16[128,256,128]{2,1,0:T(8,128)(2,1)S(1)} %bitcast.257, bf16[128,128]{1,0:T(8,128)(2,1)S(1)} %copy-done, f32[64,2,1,256,128]{4,3,1,0,2:T(8,128)} %multiply_dynamic-update-slice_fusion.4, ...), kind=kOutput, calls=%fused_computation.42 | convolution fusion | flops 1178599296 | bytes 41976832 | tf_op jit(solution)/shard_map/dot_general | solution.py:128
  279.3 11.5 %convert.2 = f32[64,2,1,256,128]{4,3,1,0,2:T(8,128)} convert(bf16[64,2,1,256,128]{4,3,1,0,2:T(8,128)(2,1)} %bitcast.230) | non-fusion elementwise | flops 4194304 | bytes 25165824 | tf_op jit(solution)/shard_map/reshape | solution.py:29
  290.8 5.8 copy-done.4
  299.5 6.9 %multiply_dynamic-update-slice_fusion.2 = f32[64,2,1,256,128]{4,3,1,0,2:T(8,128)S(1)} fusion(f32[64,2,1,256,128]{4,3,1,0,2:T(8,128)S(1)} %multiply_dynamic-update-slice_fusion.3, f32[64,2,1,256,128]{4,3,1,0,2:T(8,128)} %convert.2), kind=kLoop, calls=%fused_computation.32 | loop fusion | flops 4194304 | bytes 25165824 | tf_op jit(solution)/shard_map/scatter | solution.py:33
  320.0 5.8 copy.68
  356.3 8.8 %convolution_bitcast_fusion.7 = f32[128,128]{0,1:T(8,128)} fusion(bf16[128,256,128]{2,1,0:T(8,128)(2,1)} %get-tuple-element.783, bf16[128,256,128]{2,1,0:T(8,128)(2,1)} %param.134), kind=kOutput, calls=%fused_computation.87 | convolution fusion | flops 1073741824 | bytes 16842752 | tf_op jit(solution)/shard_map/dot_general | solution.py:67
  365.1 30.0 %psum.23 = f32[128]{0:T(128)S(1)} all-reduce(f32[128]{0:T(128)S(1)} %get-tuple-element.782), channel_id=1, replica_groups=mesh['ga'=2,'gx'=16] {'gx'}, use_global_device_ids=true, to_apply=%region_15.16 | all-reduce | flops 128 | bytes 1024 | tf_op jit(solution)/shard_map/psum | solution.py:147
  395.8 6.6 convert_element_type.60
  402.4 7.2 %fusion.43 = f32[12,128,128]{2,1,0:T(8,128)} fusion(bf16[128,256,128]{2,1,0:T(8,128)(2,1)S(1)} %convert_element_type.60, bf16[128,256,128]{2,1,0:T(8,128)(2,1)} %copy-done.9), kind=kOutput, calls=%fused_computation.76 | convolution fusion | flops 536870912 | bytes 8454144 | tf_op jit(solution)/shard_map/dot_general | solution.py:67
  434.7 7.8 %broadcast.1003 = f32[128,256,128]{2,1,0:T(8,128)} broadcast(f32[]{:T(128)} %constant.1621.clone.1), dimensions={} | broadcast | bytes 16777220 | tf_op jit(solution)/shard_map/broadcast.42
  442.5 16.3 %scatter_fusion.6 = f32[128,256,128]{2,1,0:T(8,128)} fusion(f32[128,256,128]{2,1,0:T(8,128)} %broadcast.1003, s32[64]{0:T(128)S(1)} %copy-done.14, f32[64,256,128]{2,1,0:T(8,128)} %fusion.14), kind=kCustom, calls=%fused_computation.6 | custom fusion | bytes 25166080 | tf_op jit(solution)/shard_map/scatter | solution.py:55
  458.9 8.3 %scatter_fusion.7 = f32[128,256,128]{2,1,0:T(8,128)} fusion(f32[128,256,128]{2,1,0:T(8,128)} %scatter_fusion.6, s32[32]{0:T(128)S(1)} %copy-done.16, f32[32,256,128]{2,1,0:T(8,128)} %fusion.21), kind=kCustom, calls=%fused_computation.7 | custom fusion | bytes 12583040 | tf_op jit(solution)/shard_map/scatter | solution.py:55
  498.7 82.5 %all-reduce.3.cloned.1.call-done = (f32[12,128,128]{2,1,0:T(8,128)}, f32[128,128]{0,1:T(8,128)}) async-done(((f32[12,128,128]{2,1,0:T(8,128)}, f32[128,128]{0,1:T(8,128)}), (f32[12,128,128]{2,1,0:T(8,128)}, f32[128,128]{0,1:T(8,128)})) %all-reduce.3.cloned.1.call-update) | async-done | bytes 851984 | tf_op jit(solution)/shard_map/psum | solution.py:147
  585.5 5.8 copy.88
  615.2 5.8 copy.100
  629.9 11.5 %multiply_dynamic-update-slice_fusion.1 = f32[64,2,1,256,128]{4,3,1,0,2:T(8,128)} fusion(f32[64,2,1,256,128]{4,3,1,0,2:T(8,128)} %copy.100, f32[64,1,1,256,128]{4,3,1,0,2:T(8,128)} %slice.2400), kind=kLoop, calls=%fused_computation.31 | loop fusion | flops 4194304 | bytes 25165824 | tf_op jit(solution)/shard_map/scatter | solution.py:44
  641.4 10.1 %multiply_dynamic-update-slice_fusion = f32[64,2,1,256,128]{4,3,1,0,2:T(8,128)} fusion(f32[64,2,1,256,128]{4,3,1,0,2:T(8,128)} %multiply_dynamic-update-slice_fusion.1, f32[64,2,1,256,128]{4,3,1,0,2:T(8,128)} %bitcast.223), kind=kLoop, calls=%fused_computation.30 | loop fusion | flops 4194304 | bytes 25165824 | tf_op jit(solution)/shard_map/scatter | solution.py:45
  651.5 13.9 %fusion.10 = bf16[128,256,128]{2,1,0:T(8,128)(2,1)} fusion(f32[64,2,1,256,128]{4,3,1,0,2:T(8,128)} %multiply_dynamic-update-slice_fusion, bf16[128,256,128]{2,1,0:T(8,128)(2,1)} %get-tuple-element.783, bf16[128,128]{1,0:T(8,128)(2,1)S(1)} %copy-done), kind=kOutput, calls=%fused_computation.27 | convolution fusion | flops 1082130432 | bytes 33587200 | tf_op jit(solution)/shard_map/dot_general | solution.py:154
  (260 shorter events, 268.7 us)
Async XLA Ops:
  7.2 243.2 %copy-start = (bf16[128,128]{1,0:T(8,128)(2,1)S(1)}, bf16[128,128]{1,0:T(8,128)(2,1)}, u32[]{:S(2)}) copy-start(bf16[128,128]{1,0:T(8,128)(2,1)} %param.136) | copy-start | bytes 98308
  7.2 574.1 %all-reduce.3.cloned.1.call-start = ((), (), s32[]{:S(2)}) async-start(), calls=%async_computation | async-start | bytes 1703936 | tf_op jit(solution)/shard_map/psum | solution.py:147
  73.2 1.5 collective-permute-start
  75.6 6.7 collective-permute-start.1
  78.6 46.5 %copy-start.13 = (s32[64]{0:T(128)}, s32[64]{0:T(128)S(1)}, u32[]{:S(2)}) copy-start(s32[64]{0:T(128)S(1)} %add_bitcast_fusion.5) | copy-start | bytes 772
  78.6 62.8 %copy-start.15 = (s32[32]{0:T(128)}, s32[32]{0:T(128)S(1)}, u32[]{:S(2)}) copy-start(s32[32]{0:T(128)S(1)} %add_bitcast_fusion.4) | copy-start | bytes 388
  82.4 5.1 collective-permute-start.2
  84.3 65.4 %copy-start.17 = (s32[16]{0:T(128)}, s32[16]{0:T(128)S(1)}, u32[]{:S(2)}) copy-start(s32[16]{0:T(128)S(1)} %add_bitcast_fusion.3) | copy-start | bytes 196
  84.3 69.1 %copy-start.23 = (s32[8]{0:T(128)}, s32[8]{0:T(128)S(1)}, u32[]{:S(2)}) copy-start(s32[8]{0:T(128)S(1)} %add_bitcast_fusion.2) | copy-start | bytes 100
  87.5 7.9 %collective-permute-start.3 = (f32[256,128]{1,0:T(8,128)S(1)}, f32[256,128]{1,0:T(8,128)S(1)}, u32[]{:S(2)}, u32[]{:S(2)}) collective-permute-start(f32[256,128]{1,0:T(8,128)S(1)} %select_select_fusion.8), channel_id=1, source_target_pairs={{0,8},{8,0},{1,9},{9,1},{2,10},{10,2},{3,11},{11,3},{4,12},{12,4},... | collective-permute-start | bytes 393224 | tf_op jit(solution)/shard_map/ppermute | solution.py:23
  90.4 65.9 %copy-start.19 = (s32[4]{0:T(128)}, s32[4]{0:T(128)S(1)}, u32[]{:S(2)}) copy-start(s32[4]{0:T(128)S(1)} %add_bitcast_fusion.1) | copy-start | bytes 52
  90.4 68.5 %copy-start.21 = (s32[2]{0:T(128)}, s32[2]{0:T(128)S(1)}, u32[]{:S(2)}) copy-start(s32[2]{0:T(128)S(1)} %add_bitcast_fusion) | copy-start | bytes 28
  141.4 40.9 %copy-start.26 = (bf16[128]{0:T(256)(128)(2,1)S(1)}, bf16[128]{0:T(256)(128)(2,1)}, u32[]{:S(2)}) copy-start(bf16[128]{0:T(256)(128)(2,1)} %param.138) | copy-start | bytes 772
  164.7 7.4 %collective-permute-start.4 = (f32[256,128]{1,0:T(8,128)S(1)}, f32[256,128]{1,0:T(8,128)S(1)}, u32[]{:S(2)}, u32[]{:S(2)}) collective-permute-start(f32[256,128]{1,0:T(8,128)S(1)} %get-tuple-element.779), channel_id=1, source_target_pairs={{0,8},{8,0},{1,9},{9,1},{2,10},{10,2},{3,11},{11,3},{4,12},{12,4},... | collective-permute-start | bytes 393224 | tf_op jit(solution)/shard_map/ppermute | solution.py:23
  172.1 5.0 collective-permute-start.5
  177.2 5.0 collective-permute-start.6
  182.2 1.4 collective-permute-start.7
  228.5 21.9 %slice-start.4 = ((s8[8388608]{0:T(1024)(128)(4,1)}), s8[4194304]{0:T(1024)(128)(4,1)S(1)}, s32[]{:S(2)}) async-start(s8[8388608]{0:T(1024)(128)(4,1)} %bitcast.256), calls=%async_computation.5 | async-start | bytes 8388608
  339.5 1.4 collective-permute-start.8
  345.2 5.6 collective-permute-start.9
  350.9 5.0 collective-permute-start.10
  351.2 66.8 %copy-start.12 = (bf16[12,128,128]{1,2,0:T(8,128)(2,1)}, bf16[12,128,128]{1,2,0:T(8,128)(2,1)S(1)}, u32[]{:S(2)}) copy-start(bf16[12,128,128]{1,2,0:T(8,128)(2,1)S(1)} %copy.10) | copy-start | bytes 1179652
  355.9 39.2 %collective-permute-start.11 = (f32[256,128]{1,0:T(8,128)S(1)}, f32[256,128]{1,0:T(8,128)S(1)}, u32[]{:S(2)}, u32[]{:S(2)}) collective-permute-start(f32[256,128]{1,0:T(8,128)S(1)} %select_select_fusion.3), channel_id=1, source_target_pairs={{0,8},{8,0},{1,9},{9,1},{2,10},{10,2},{3,11},{11,3},{4,12},{12,4},... | collective-permute-start | bytes 393224 | tf_op jit(solution)/shard_map/ppermute | solution.py:23
  402.4 30.6 %copy-start.10 = (bf16[128,256,128]{2,1,0:T(8,128)(2,1)}, bf16[128,256,128]{2,1,0:T(8,128)(2,1)S(1)}, u32[]{:S(2)}) copy-start(bf16[128,256,128]{2,1,0:T(8,128)(2,1)S(1)} %convert_element_type.60) | copy-start | bytes 25165828
  417.9 24.6 %copy-start.14 = (s32[64]{0:T(128)S(1)}, s32[64]{0:T(128)}, u32[]{:S(2)}) copy-start(s32[64]{0:T(128)} %copy-done.13) | copy-start | bytes 772
  442.5 24.7 %copy-start.18 = (s32[16]{0:T(128)S(1)}, s32[16]{0:T(128)}, u32[]{:S(2)}) copy-start(s32[16]{0:T(128)} %copy-done.17) | copy-start | bytes 196
  442.5 28.3 %copy-start.24 = (s32[8]{0:T(128)S(1)}, s32[8]{0:T(128)}, u32[]{:S(2)}) copy-start(s32[8]{0:T(128)} %copy-done.23) | copy-start | bytes 100
  458.9 124.0 %copy-start.25 = (f32[12]{0:T(128)S(1)}, f32[12]{0:T(128)}, u32[]{:S(2)}) copy-start(f32[12]{0:T(128)} %constant.1644.clone) | copy-start | bytes 148
  481.9 5.9 collective-permute-start.12
  487.8 5.0 collective-permute-start.13
  492.9 5.7 collective-permute-start.14
  498.7 86.2 %collective-permute-start.15 = (f32[256,128]{1,0:T(8,128)S(1)}, f32[256,128]{1,0:T(8,128)S(1)}, u32[]{:S(2)}, u32[]{:S(2)}) collective-permute-start(f32[256,128]{1,0:T(8,128)S(1)} %select_select_fusion), channel_id=1, source_target_pairs={{0,1},{1,0},{2,3},{3,2},{4,5},{5,4},{6,7},{7,6},{8,9},{9,8},{10,11... | collective-permute-start | bytes 393224 | tf_op jit(solution)/shard_map/ppermute | solution.py:23
  (18 other events, 178.9 us)
Sparse Core Ops, SparseCore 0:
  490.2 90.9 all-reduce.2
where the time goes:
time: 684 us; the launch traced here: 673 us
  local copies, waits for them, and re-layouts  227 us (33%)
  other arithmetic  148 us (22%)
  waiting for transfers between devices  135 us (20%)
  matrix products  105 us (15%)
  blocking collectives  30 us (4%)
  between operations  15.4 us (2%)
  starting transfers between devices  12.5 us (2%)
    unnamed x95, local copies, waits for them, and re-layouts  123 us
    psum x1, waiting for transfers between devices, shards(): totals = lax.psum((stacked, point_grad, bias_grad), 'gx')  82.5 us
    scatter x12, local copies, waits for them, and re-layouts, mix_levels(): output.at[stride::2 * stride]  72.3 us
    ppermute x16, waiting for transfers between devices, partner_2(): return lax.ppermute(block, axis, route)  52.4 us
    scatter x14, other arithmetic, haar_inverse(): shaped = shaped.at[:, 1, 0].set((coarse_rows + detail_rows) * root_half)  31.5 us
    psum x1, blocking collectives, shards(): totals = lax.psum((stacked, point_grad, bias_grad), 'gx')  30 us
    scatter x14, other arithmetic, haar_inverse(): shaped = shaped.at[:, 0, 0].set((coarse_rows - detail_rows) * root_half)  29.8 us
    dot_general x9, matrix products, outer_sum(): lax.dot_general(left_flat, right_flat, (((0,), (0,)), ((), ())), preferre...  29.6 us
  transfers between devices with their start and end apart: 17, of which 15 were waited for; matrix products, arithmetic and copies ran while one was open for 2% of the time, Pallas kernels for 0%

commit v1 on v0

v1 whole, which is shorter than its diff:
```python
import functools
import math

import jax
import jax.numpy as jnp
import numpy as np
from jax import lax
from jax.experimental import pallas as pl
from jax.experimental.pallas import tpu as pltpu
from jax.sharding import PartitionSpec as P

F32 = jnp.float32
BF16 = jnp.bfloat16
LANES = 16
GELU_K = math.sqrt(2.0 / math.pi)
GELU_C = 0.044715


def offset(rows, level):
    return rows - (rows >> level)


def outer(left, right):
    return lax.dot_general(left, right, (((0,), (0,)), ((), ())), preferred_element_type=F32)


def slope_of(value, cot):
    square = value * value
    inner = value * (GELU_K + (GELU_K * GELU_C) * square)
    half = 0.5 + 0.5 * jnp.tanh(inner)
    ramp = value * (2.0 * GELU_K + (6.0 * GELU_K * GELU_C) * square)
    return cot * (half * (1.0 + (1.0 - half) * ramp))


def analyse_kernel(depth, fields_ref, coeff_ref, coarse_ref):
    rows = 1 << depth

    @pl.loop(0, fields_ref.shape[1] // LANES)
    def _(sub):
        cols = pl.ds(pl.multiple_of(sub * LANES, LANES), LANES)

        def tree(level, index):
            if level == 0:
                return fields_ref[index, cols, :].astype(F32)
            even = tree(level - 1, 2 * index)
            odd = tree(level - 1, 2 * index + 1)
            coeff_ref[0, offset(rows, level - 1) + index, cols, :] = (odd - even).astype(BF16)
            return even + odd

        coarse_ref[cols, :] = tree(depth, 0)


def mix_block(depth, coeff_ref, weight_ref, mixed_ref):
    rows = 1 << depth
    wide = coeff_ref.shape[2]
    for level in range(depth):
        first, count = offset(rows, level), rows >> (level + 1)
        flat = coeff_ref[0, first : first + count].reshape(count * wide, coeff_ref.shape[3])
        mixed_ref[first : first + count] = jnp.dot(
            flat, weight_ref[level], preferred_element_type=F32
        ).reshape(count, wide, weight_ref.shape[2])


def middle_kernel(
    depth, coeff_ref, cot_ref, coarse_ref, weight_ref, bias_ref, back_ref, sums_ref, grad_ref, mixed_ref
):
    rows = 1 << depth
    wide = coeff_ref.shape[2]
    mix_block(depth, coeff_ref, weight_ref, mixed_ref)

    @pl.loop(0, wide // LANES)
    def _(sub):
        cols = pl.ds(pl.multiple_of(sub * LANES, LANES), LANES)

        def tree(level, index, value):
            if level == 0:
                cot = cot_ref[index, cols, :].astype(F32)
                return slope_of(value, cot).astype(BF16).astype(F32)
            place = offset(rows, level - 1) + index
            detail = mixed_ref[place, cols, :]
            even = tree(level - 1, 2 * index, value - detail)
            odd = tree(level - 1, 2 * index + 1, value + detail)
            back_ref[0, place, cols, :] = (odd - even).astype(BF16)
            return even + odd

        sums_ref[cols, :] = tree(depth, 0, coarse_ref[cols, :] + bias_ref[0:1, :])

    @pl.when(pl.program_id(0) == 0)
    def _():
        grad_ref[...] = jnp.zeros_like(grad_ref)

    for level in range(depth):
        first, count = offset(rows, level), rows >> (level + 1)
        left = coeff_ref[0, first : first + count].reshape(count * wide, coeff_ref.shape[3])
        right = back_ref[0, first : first + count].reshape(count * wide, coeff_ref.shape[3])
        grad_ref[level] += outer(left, right)


def synth_kernel(depth, back_ref, coarse_ref, weight_ref, out_ref, mixed_ref):
    rows = 1 << depth
    mix_block(depth, back_ref, weight_ref, mixed_ref)

    @pl.loop(0, back_ref.shape[2] // LANES)
    def _(sub):
        cols = pl.ds(pl.multiple_of(sub * LANES, LANES), LANES)

        def tree(level, index, value):
            if level == 0:
                out_ref[index, cols, :] = value.astype(BF16)
                return
            detail = mixed_ref[offset(rows, level - 1) + index, cols, :]
            tree(level - 1, 2 * index, value - detail)
            tree(level - 1, 2 * index + 1, value + detail)

        tree(depth, 0, coarse_ref[cols, :])


def cross_kernel(
    count, with_grad, coarse_ref, weight_ref, other_ref, out_ref, coeff_ref, grad_ref,
    arrived, leaving, landed, send_a, recv_a, send_b, recv_b,
):
    me = lax.axis_index("gx")
    depth = count.bit_length() - 1
    cols, chans = coarse_ref.shape[1], coarse_ref.shape[2]
    barrier = pltpu.get_barrier_semaphore()

    def peer(step):
        return lax.rem(me + step, count)

    @pl.loop(1, count)
    def _(step):
        pl.semaphore_signal(
            barrier, inc=1, device_id={"gx": peer(step)}, device_id_type=pl.DeviceIdType.MESH
        )

    pl.semaphore_wait(barrier, count - 1)

    def swap(source, target, send, recv, step):
        return pltpu.make_async_remote_copy(
            src_ref=source.at[peer(step)],
            dst_ref=target.at[me],
            send_sem=send.at[step],
            recv_sem=recv.at[step],
            device_id={"gx": peer(step)},
            device_id_type=pl.DeviceIdType.MESH,
        )

    def exchange(source, target, send, recv):
        @pl.loop(1, count)
        def _(step):
            swap(source, target, send, recv, step).start()

        target[me] = source[me]

        @pl.loop(1, count)
        def _(step):
            swap(source, target, send, recv, step).wait()

    exchange(coarse_ref, arrived, send_a, recv_a)

    def down(level, index):
        if level == 0:
            return arrived[index]
        even = down(level - 1, 2 * index)
        odd = down(level - 1, 2 * index + 1)
        coeff_ref[offset(count, level - 1) + index] = (odd - even).astype(BF16)
        return even + odd

    coeff_ref[count - 1] = down(depth, 0).astype(BF16)
    mixed = []
    for level in range(depth + 1):
        first = offset(count, level)
        total = max(count >> (level + 1), 1)
        flat = coeff_ref[first : first + total].astype(F32).reshape(total * cols, chans).astype(BF16)
        mixed.append(
            jnp.dot(flat, weight_ref[level], preferred_element_type=F32).reshape(total, cols, chans)
        )
        if with_grad:
            prior = other_ref[first : first + total].astype(F32).reshape(total * cols, chans)
            grad_ref[level] = outer(prior.astype(BF16), flat)

    def up(level, index, value):
        if level == 0:
            leaving[index] = value
            return
        detail = mixed[level - 1][index]
        up(level - 1, 2 * index, value - detail)
        up(level - 1, 2 * index + 1, value + detail)

    up(depth, 0, mixed[depth][0])
    exchange(leaving, landed, send_b, recv_b)
    out_ref[...] = landed[...]


def cross(coarse, weights, other, with_grad, identity):
    count, cols, chans = coarse.shape
    levels = weights.shape[0]
    grad_shape = (levels if with_grad else 1, 8 if not with_grad else chans, chans)
    whole = pl.BlockSpec(memory_space=pltpu.VMEM)
    return pl.pallas_call(
        functools.partial(cross_kernel, count, with_grad),
        out_shape=(
            jax.ShapeDtypeStruct(coarse.shape, F32),
            jax.ShapeDtypeStruct(coarse.shape, BF16),
            jax.ShapeDtypeStruct(grad_shape, F32),
        ),
        in_specs=[whole] * 3,
        out_specs=(whole,) * 3,
        scratch_shapes=[pltpu.VMEM(coarse.shape, F32)] * 3 + [pltpu.SemaphoreType.DMA((count,))] * 4,
        compiler_params=pltpu.CompilerParams(
            collective_id=identity, has_side_effects=True, vmem_limit_bytes=32 << 20
        ),
    )(coarse, weights, other)


def shards(fields, cotangent, point_weight, mix_weight, bias_vec):
    rows, width, chans = fields.shape
    depth = rows.bit_length() - 1
    count = lax.axis_size("gx")
    levels = mix_weight.shape[0]
    step = 32
    blocks = width // step
    scales = [2.0 ** -(level + 1) for level in range(levels - 1)] + [2.0 ** -(levels - 1)]
    scales = np.array(scales, np.float32)
    joined = mix_weight.astype(F32) + point_weight.astype(F32)[None]
    weights = (joined * scales[:, None, None]).astype(BF16)
    turned = jnp.swapaxes(weights, 1, 2)
    bias = jnp.broadcast_to(bias_vec.astype(F32)[None], (8, chans))

    field_spec = pl.BlockSpec((rows, step, chans), lambda i: (0, i, 0))
    coeff_spec = pl.BlockSpec((1, rows, step, chans), lambda i: (i, 0, 0, 0))
    row_spec = pl.BlockSpec((step, chans), lambda i: (i, 0))
    weight_spec = pl.BlockSpec((depth, chans, chans), lambda i: (0, 0, 0))
    params = pltpu.CompilerParams(
        dimension_semantics=("arbitrary",), vmem_limit_bytes=48 << 20
    )
    coeff_type = jax.ShapeDtypeStruct((blocks, rows, step, chans), BF16)
    row_type = jax.ShapeDtypeStruct((width, chans), F32)
    mixed_type = pltpu.VMEM((rows, step, chans), F32)

    coeffs, coarse = pl.pallas_call(
        functools.partial(analyse_kernel, depth),
        grid=(blocks,),
        in_specs=[field_spec],
        out_specs=(coeff_spec, row_spec),
        out_shape=(coeff_type, row_type),
        compiler_params=params,
    )(fields)

    far_shape = (count, width // count, chans)
    local_w, far_w = weights[:depth], weights[depth:]
    local_t, far_t = turned[:depth], turned[depth:]
    spectral, far_coeffs, _ = cross(
        coarse.reshape(far_shape), far_w, jnp.zeros((1, 16, chans), BF16), False, 0
    )

    backs, sums, grad_local = pl.pallas_call(
        functools.partial(middle_kernel, depth),
        grid=(blocks,),
        in_specs=[
            coeff_spec, field_spec, row_spec, weight_spec,
            pl.BlockSpec((8, chans), lambda i: (0, 0)),
        ],
        out_specs=(coeff_spec, row_spec, weight_spec),
        out_shape=(coeff_type, row_type, jax.ShapeDtypeStruct((depth, chans, chans), F32)),
        scratch_shapes=[mixed_type],
        compiler_params=params,
    )(coeffs, cotangent, spectral.reshape(width, chans), local_w, bias)

    spectral_back, _, grad_far = cross(sums.reshape(far_shape), far_t, far_coeffs, True, 1)

    bias_local = jnp.sum(sums.reshape(width // 8, 8, chans), axis=0)
    grads = jnp.concatenate([grad_local, grad_far], axis=0).reshape(levels * chans, chans)
    totals = lax.psum(jnp.concatenate([grads, bias_local], axis=0), "gx")

    (grad_input,) = pl.pallas_call(
        functools.partial(synth_kernel, depth),
        grid=(blocks,),
        in_specs=[coeff_spec, row_spec, weight_spec],
        out_specs=(field_spec,),
        out_shape=(jax.ShapeDtypeStruct(fields.shape, BF16),),
        scratch_shapes=[mixed_type],
        compiler_params=params,
        cost_estimate=pl.CostEstimate(
            flops=2 * rows * width * chans * chans, bytes_accessed=4 * rows * width * chans,
            transcendentals=0,
        ),
    )(backs, spectral_back.reshape(width, chans), local_t)

    total_rows = rows * count
    raw = totals[: levels * chans].reshape(levels, chans, chans) * scales[:, None, None]
    members = [width * total_rows / 2 ** (level + 1) for level in range(levels - 1)] + [width]
    factors = np.array([1.0 / math.sqrt(value) for value in members], np.float32)
    scale_all = 1.0 / math.sqrt(total_rows * width)
    grad_mix = (raw * factors[:, None, None]).astype(BF16)
    grad_point = (jnp.sum(raw, axis=0) * scale_all).astype(BF16)
    grad_bias = (jnp.sum(totals[levels * chans :], axis=0) * scale_all).astype(BF16)
    return (grad_input, grad_mix, grad_point, grad_bias)


def solution(mesh):
    in_specs = (P("gx", "ga", None), P("gx", "ga", None), P(), P(), P())
    out_specs = (P("gx", "ga", None), P("ga", None, None), P("ga", None), P("ga"))
    return jax.shard_map(shards, mesh=mesh, in_specs=in_specs, out_specs=out_specs, check_vma=False)
```

time: 684 us -> 178 us (0.26); the launches traced: 673 us -> 177 us
  local copies, waits for them, and re-layouts: 227 us -> 5.6 us
  other arithmetic: 148 us -> 4.04 us
  matrix products: 105 us -> 0 us
  Pallas kernels: 0 us -> 72.6 us
  waiting for transfers between devices: 135 us -> 80.7 us
  blocking collectives: 30 us -> 0 us
  starting transfers between devices: 12.5 us -> 0.04 us
    unnamed x95 -> x9, local copies, waits for them, and re-layouts: 123 us -> 2.89 us
    dot_general x27 -> x0, matrix products: 105 us -> none  [the longest x9 29.6 us: outer_sum(): lax.dot_general(left_flat, right_flat, (((0,), (0,)), ((), ())), preferre...]
    scatter x60 -> x0, other arithmetic: 105 us -> none  [the longest x14 31.5 us: haar_inverse(): shaped = shaped.at[:, 1, 0].set((coarse_rows + detail_rows) * root_half)]
    pallas_call x0 -> x5, Pallas kernels: none -> 72.6 us  [the longest x2 30.3 us: cross(): pl.pallas_call(functools.partial(cross_kernel, count, with_grad), out_sha...]
    scatter x12 -> x0, local copies, waits for them, and re-layouts: 72.3 us -> none  [mix_levels(): output.at[stride::2 * stride]]
    ppermute x16 -> x0, waiting for transfers between devices: 52.4 us -> none  [partner_2(): return lax.ppermute(block, axis, route)]
    psum x1 -> x0, blocking collectives: 30 us -> none  [shards(): totals = lax.psum((stacked, point_grad, bias_grad), 'gx')]
    reshape x2 -> x0, other arithmetic: 23.1 us -> none  [haar_forward(): signal.reshape((signal.shape[0] // (2 * stride), 2, stride) + signal.shap...]
  transfers between devices with their start and end apart: 17 -> 1, of which waited for: 15 -> 1; matrix products, arithmetic and copies ran while one was open for 2% -> 0% of each run, Pallas kernels for 0% -> 6%
where the time goes in v1:
time: 178 us; the launch traced here: 177 us
  waiting for transfers between devices  80.7 us (45%)
  Pallas kernels  72.6 us (41%)
  between operations  14.2 us (8%)
  local copies, waits for them, and re-layouts  5.6 us (3%)
  other arithmetic  4.04 us (2%)
    psum x1, waiting for transfers between devices, shards(): totals = lax.psum(jnp.concatenate([grads, bias_local], axis=0), 'gx')  80.7 us
    pallas_call x2, Pallas kernels, cross(): pl.pallas_call(functools.partial(cross_kernel, count, with_grad), out_sha...  30.3 us
    pallas_call x1, Pallas kernels, shards(): pl.pallas_call(functools.partial(middle_kernel, depth), grid=(blocks,), i...  22 us
    pallas_call x1, Pallas kernels, shards(): pl.pallas_call(functools.partial(synth_kernel, depth), grid=(blocks,), in...  10.6 us
    pallas_call x1, Pallas kernels, shards(): pl.pallas_call(functools.partial(analyse_kernel, depth), grid=(blocks,),...  9.64 us
  transfers between devices with their start and end apart: 1, of which 1 were waited for; matrix products, arithmetic and copies ran while one was open for 0% of the time, Pallas kernels for 6%

profile of v1, /device:TPU:0, one launch (start us, length us, event | category | flops | bytes accessed | tf_op | source)
XLA Modules:
  0.0 177.1 jit_solution(12579441264881505273)
XLA Ops:
  7.2 0.0 copy-start.2
  7.2 0.0 all-reduce.2.cloned.1.call-start
  7.2 0.8 copy.24
  8.1 1.2 copy.23
  9.3 0.8 fusion
  10.1 0.8 multiply_convert_fusion.1
  10.9 0.2 copy.26.weight_ref
  11.1 0.2 copy.25.weight_ref
  11.3 9.6 %shard_map.111 = (bf16[8,128,32,128]{3,2,1,0:T(8,128)(2,1)}, f32[256,128]{1,0:T(8,128)S(1)}) custom-call(bf16[128,256,128]{2,1,0:T(8,128)(2,1)} %fields_ref.1), custom_call_target="tpu_custom_call" | custom-call | tf_op jit(solution)/shard_map/pallas_call | solution.py:241
  21.0 16.9 %shard_map.112 = (f32[16,16,128]{2,1,0:T(8,128)S(1)}, bf16[16,16,128]{2,1,0:T(8,128)(2,1)S(1)}, f32[1,8,128]{2,1,0:T(8,128)}) custom-call(f32[16,16,128]{2,1,0:T(8,128)S(1)} %bitcast.13, bf16[5,128,128]{2,1,0:T(8,128)(2,1)S(1)} %copy.25.weight_ref, bf16[1,16,128]{2,1,0:T(8,128)(2,1)S(1)} %broadcast_in_dim.4.other_ref), custom_call_target="tpu_custom_call" | custom-call | tf_op jit(solution)/shard_map/pallas_call | solution.py:200
  37.9 0.0 copy-done.2
  37.9 22.0 %shard_map.113 = (bf16[8,128,32,128]{3,2,1,0:T(8,128)(2,1)}, f32[256,128]{1,0:T(8,128)S(1)}, f32[7,128,128]{2,1,0:T(8,128)S(1)}) custom-call(bf16[8,128,32,128]{3,2,1,0:T(8,128)(2,1)} %get-tuple-element.13.coeff_ref, bf16[128,256,128]{2,1,0:T(8,128)(2,1)} %cot_ref.1, f32[256,128]{1,0:T(8,128)S(1)} %bitcast.12, bf16[7,128,128]{2,1,0:T(8,128)(2,1)S(1)} %copy.26.weight_ref, ...), custom_call_target="tpu_custom_call" | custom-call | tf_op jit(solution)/shard_map/pallas_call | solution.py:257
  59.9 13.4 %shard_map.114 = (f32[16,16,128]{2,1,0:T(8,128)S(1)}, bf16[16,16,128]{2,1,0:T(8,128)(2,1)}, f32[5,128,128]{2,1,0:T(8,128)S(1)}) custom-call(f32[16,16,128]{2,1,0:T(8,128)S(1)} %bitcast.10, bf16[5,128,128]{2,1,0:T(8,128)(2,1)S(1)} %slice.26.weight_ref, bf16[16,16,128]{2,1,0:T(8,128)(2,1)S(1)} %get-tuple-element.18.other_ref), custom_call_target="tpu_custom_call" | custom-call | tf_op jit(solution)/shard_map/pallas_call | solution.py:200
  73.3 0.1 pad_maximum_fusion.1
  73.4 1.0 pad_maximum_fusion
  74.4 0.0 all-reduce.2.cloned.1.call-update
  74.4 0.0 copy-start
  74.4 0.0 copy-start.1
  74.4 10.6 %shard_map.115 = bf16[128,256,128]{2,1,0:T(8,128)(2,1)} custom-call(bf16[8,128,32,128]{3,2,1,0:T(8,128)(2,1)} %get-tuple-element.16.back_ref, f32[256,128]{1,0:T(8,128)S(1)} %bitcast.11, bf16[7,128,128]{2,1,0:T(8,128)(2,1)S(1)} %slice.27.weight_ref), custom_call_target="tpu_custom_call" | custom-call | flops 1073741824 | bytes 16777216 | tf_op jit(solution)/shard_map/pallas_call | solution.py:276
  85.0 80.7 %all-reduce.2.cloned.1.call-done = f32[1544,128]{1,0:T(8,128)} async-done(((f32[1544,128]{1,0:T(8,128)}), f32[1544,128]{1,0:T(8,128)}) %all-reduce.2.cloned.1.call-update) | async-done | bytes 790544 | tf_op jit(solution)/shard_map/psum | solution.py:274
  165.7 1.2 slice.28
  166.9 0.3 copy.27
  167.2 0.0 copy-done
  167.2 0.0 copy-done.1
  167.2 0.2 multiply_reduce_fusion
  167.4 0.7 copy.29
  168.1 0.7 slice_reduce_fusion
  168.8 0.5 multiply_convert_fusion.3
  169.3 0.9 copy.28
  (8 shorter events, 0.1 us)
Async XLA Ops:
  7.2 30.7 %copy-start.2 = (bf16[128]{0:T(256)(128)(2,1)S(1)}, bf16[128]{0:T(256)(128)(2,1)}, u32[]{:S(2)}) copy-start(bf16[128]{0:T(256)(128)(2,1)} %param.12) | copy-start | bytes 772
  7.2 158.5 %all-reduce.2.cloned.1.call-start = ((), (), s32[]{:S(2)}) async-start(), calls=%async_computation | async-start | bytes 1581056 | tf_op jit(solution)/shard_map/psum | solution.py:274
  74.4 92.8 %copy-start = (f32[12]{0:T(128)S(1)}, f32[12]{0:T(128)}, u32[]{:S(2)}) copy-start(f32[12]{0:T(128)} %constant.13) | copy-start | bytes 148
  74.4 92.8 %copy-start.1 = (f32[12]{0:T(128)S(1)}, f32[12]{0:T(128)}, u32[]{:S(2)}) copy-start(f32[12]{0:T(128)} %constant.14) | copy-start | bytes 148
Sparse Core Ops, SparseCore 0:
  74.5 91.1 all-reduce.1

commit v2 on v1

v2 whole, which is shorter than its diff:
```python
import functools
import math

import jax
import jax.numpy as jnp
import numpy as np
from jax import lax
from jax.experimental import pallas as pl
from jax.experimental.pallas import tpu as pltpu
from jax.sharding import PartitionSpec as P

F32 = jnp.float32
BF16 = jnp.bfloat16
LANES = 16
GELU_K = math.sqrt(2.0 / math.pi)
GELU_C = 0.044715


def offset(rows, level):
    return rows - (rows >> level)


def outer(left, right):
    return lax.dot_general(left, right, (((0,), (0,)), ((), ())), preferred_element_type=F32)


def apply_weight(rows, weight, turned):
    sides = (((1,), (1 if turned else 0,)), ((), ()))
    return lax.dot_general(rows, weight, sides, preferred_element_type=F32)


def slope_of(value, cot):
    square = value * value
    inner = value * (GELU_K + (GELU_K * GELU_C) * square)
    half = 0.5 + 0.5 * jnp.tanh(inner)
    ramp = value * (2.0 * GELU_K + (6.0 * GELU_K * GELU_C) * square)
    return cot * (half * (1.0 + (1.0 - half) * ramp))


def analyse_kernel(depth, fields_ref, coeff_ref, coarse_ref):
    rows = 1 << depth

    @pl.loop(0, fields_ref.shape[1] // LANES)
    def _(sub):
        cols = pl.ds(pl.multiple_of(sub * LANES, LANES), LANES)

        def tree(level, index):
            if level == 0:
                return fields_ref[index, cols, :].astype(F32)
            even = tree(level - 1, 2 * index)
            odd = tree(level - 1, 2 * index + 1)
            coeff_ref[0, offset(rows, level - 1) + index, cols, :] = (odd - even).astype(BF16)
            return even + odd

        coarse_ref[cols, :] = tree(depth, 0)


def mix_block(depth, coeff_ref, weight_ref, mixed_ref, turned):
    rows = 1 << depth
    wide = coeff_ref.shape[2]
    for level in range(depth):
        first, count = offset(rows, level), rows >> (level + 1)
        flat = coeff_ref[0, first : first + count].reshape(count * wide, coeff_ref.shape[3])
        mixed_ref[first : first + count] = apply_weight(flat, weight_ref[level], turned).reshape(
            count, wide, weight_ref.shape[2]
        )


def middle_kernel(
    depth, coeff_ref, cot_ref, coarse_ref, weight_ref, bias_ref, back_ref, sums_ref, grad_ref, mixed_ref
):
    rows = 1 << depth
    wide = coeff_ref.shape[2]
    mix_block(depth, coeff_ref, weight_ref, mixed_ref, False)

    @pl.loop(0, wide // LANES)
    def _(sub):
        cols = pl.ds(pl.multiple_of(sub * LANES, LANES), LANES)

        def tree(level, index, value):
            if level == 0:
                cot = cot_ref[index, cols, :].astype(F32)
                return slope_of(value, cot).astype(BF16).astype(F32)
            place = offset(rows, level - 1) + index
            detail = mixed_ref[place, cols, :]
            even = tree(level - 1, 2 * index, value - detail)
            odd = tree(level - 1, 2 * index + 1, value + detail)
            back_ref[0, place, cols, :] = (odd - even).astype(BF16)
            return even + odd

        sums_ref[cols, :] = tree(depth, 0, coarse_ref[cols, :] + bias_ref[0:1, :])

    @pl.when(pl.program_id(0) == 0)
    def _():
        grad_ref[...] = jnp.zeros_like(grad_ref)

    for level in range(depth):
        first, count = offset(rows, level), rows >> (level + 1)
        left = coeff_ref[0, first : first + count].reshape(count * wide, coeff_ref.shape[3])
        right = back_ref[0, first : first + count].reshape(count * wide, coeff_ref.shape[3])
        grad_ref[level] += outer(left, right)


def synth_kernel(depth, back_ref, coarse_ref, weight_ref, out_ref, mixed_ref):
    rows = 1 << depth
    mix_block(depth, back_ref, weight_ref, mixed_ref, True)

    @pl.loop(0, back_ref.shape[2] // LANES)
    def _(sub):
        cols = pl.ds(pl.multiple_of(sub * LANES, LANES), LANES)

        def tree(level, index, value):
            if level == 0:
                out_ref[index, cols, :] = value.astype(BF16)
                return
            detail = mixed_ref[offset(rows, level - 1) + index, cols, :]
            tree(level - 1, 2 * index, value - detail)
            tree(level - 1, 2 * index + 1, value + detail)

        tree(depth, 0, coarse_ref[cols, :])


class Stream:
    def __init__(self, total, slots, result, send, recv, bits, me):
        self.total, self.slots, self.result = total, slots, result
        self.send, self.recv = send, recv
        start, length, place = 0, total.shape[0], 0
        self.plan = []
        for turn, bit in enumerate(bits):
            upper = lax.rem(me // (1 << bit), 2)
            partner = me + (1 - 2 * upper) * (1 << bit)
            halved = length % 2 == 0
            size = length // 2 if halved else length
            keep = start + upper * size if halved else start
            give = start + (1 - upper) * size if halved else start
            self.plan.append((turn, partner, halved, size, keep, give, place))
            start, length, place = keep, size, place + size
        self.stages = [("sum",) + item for item in self.plan]
        self.stages += [("spread",) + item for item in self.plan[::-1] if item[2]]

    def copy(self, index):
        kind, turn, partner, halved, size, keep, give, place = self.stages[index]
        if kind == "sum":
            source = self.total.at[pl.ds(give, size)]
            target = self.slots.at[pl.ds(place, size)]
        else:
            source = self.result.at[pl.ds(keep, size)]
            target = self.result.at[pl.ds(keep, size)]
        return pltpu.make_async_remote_copy(
            src_ref=source,
            dst_ref=target,
            send_sem=self.send.at[index],
            recv_sem=self.recv.at[index],
            device_id={"gx": partner},
            device_id_type=pl.DeviceIdType.MESH,
        )

    def start(self, index):
        if index < len(self.stages):
            self.copy(index).start()

    def finish(self, index):
        self.copy(index).wait()
        kind, turn, partner, halved, size, keep, give, place = self.stages[index]
        if kind == "sum":
            here = pl.ds(keep, size)
            into = self.result if turn == len(self.plan) - 1 else self.total
            into[here] = self.total[here] + self.slots[pl.ds(place, size)]


def slot_tiles(tiles, count):
    used = 0
    for _ in range(count.bit_length() - 1):
        tiles = tiles // 2 if tiles % 2 == 0 else tiles
        used += tiles
    return used


def far_levels(count, first_level, arrived, coeff_ref, weight_ref, turned):
    depth = count.bit_length() - 1
    cols, chans = arrived.shape[1], arrived.shape[2]

    def down(level, index):
        if level == 0:
            return arrived[index]
        even = down(level - 1, 2 * index)
        odd = down(level - 1, 2 * index + 1)
        coeff_ref[offset(count, level - 1) + index] = (odd - even).astype(BF16)
        return even + odd

    coeff_ref[count - 1] = down(depth, 0).astype(BF16)
    mixed, flats = [], []
    for level in range(depth + 1):
        first = offset(count, level)
        total = max(count >> (level + 1), 1)
        flat = coeff_ref[first : first + total].astype(F32).reshape(total * cols, chans).astype(BF16)
        flats.append(flat)
        mixed.append(
            apply_weight(flat, weight_ref[first_level + level], turned).reshape(total, cols, chans)
        )
    return mixed, flats


def far_back(count, mixed, leaving, cols):
    depth = count.bit_length() - 1

    def up(level, index, value):
        if level == 0:
            leaving[index, 0:cols] = value
            return
        detail = mixed[level - 1][index]
        up(level - 1, 2 * index, value - detail)
        up(level - 1, 2 * index + 1, value + detail)

    up(depth, 0, mixed[depth][0])


def greet(count, me):
    barrier = pltpu.get_barrier_semaphore()

    @pl.loop(1, count)
    def _(step):
        pl.semaphore_signal(
            barrier,
            inc=1,
            device_id={"gx": lax.rem(me + step, count)},
            device_id_type=pl.DeviceIdType.MESH,
        )

    pl.semaphore_wait(barrier, count - 1)


def swap(count, me, source, target, send, recv, step):
    peer = lax.rem(me + step, count)
    return pltpu.make_async_remote_copy(
        src_ref=source.at[peer],
        dst_ref=target.at[me],
        send_sem=send.at[step],
        recv_sem=recv.at[step],
        device_id={"gx": peer},
        device_id_type=pl.DeviceIdType.MESH,
    )


def exchange_start(count, me, source, target, send, recv):
    @pl.loop(1, count)
    def _(step):
        swap(count, me, source, target, send, recv, step).start()

    target[me] = source[me]


def exchange_wait(count, me, source, target, send, recv):
    @pl.loop(1, count)
    def _(step):
        swap(count, me, source, target, send, recv, step).wait()


def cross_kernel(
    count, first_level, coarse_ref, weight_ref, out_ref, coeff_ref,
    arrived, leaving, landed, send_a, recv_a, send_b, recv_b,
):
    me = lax.axis_index("gx")
    greet(count, me)
    exchange_start(count, me, coarse_ref, arrived, send_a, recv_a)
    exchange_wait(count, me, coarse_ref, arrived, send_a, recv_a)
    mixed, _ = far_levels(count, first_level, arrived, coeff_ref, weight_ref, False)
    far_back(count, mixed, leaving, coarse_ref.shape[1])
    exchange_start(count, me, leaving, landed, send_b, recv_b)
    exchange_wait(count, me, leaving, landed, send_b, recv_b)
    out_ref[...] = landed[...]


def cross_back_kernel(
    count, first_level, factors, scales, scale_all, coarse_ref, weight_ref, other_ref, local_ref,
    out_ref, mix_ref, point_ref, bias_ref,
    coeff_ref, arrived, leaving, landed, near, near_slots, near_sum, far, far_slots, far_sum,
    send_a, recv_a, send_b, recv_b, send_n, recv_n, send_f, recv_f,
):
    me = lax.axis_index("gx")
    cols, chans = coarse_ref.shape[1], coarse_ref.shape[2]
    tiles = chans // 8
    bits = list(range(count.bit_length() - 1))
    greet(count, me)
    exchange_start(count, me, coarse_ref, arrived, send_a, recv_a)
    near[...] = local_ref[...]
    streams = [Stream(near, near_slots, near_sum, send_n, recv_n, bits, me)]
    streams.append(Stream(far, far_slots, far_sum, send_f, recv_f, bits[:1] + bits[2:] + bits[1:2], me))
    streams[0].start(0)
    exchange_wait(count, me, coarse_ref, arrived, send_a, recv_a)
    mixed, flats = far_levels(count, first_level, arrived, coeff_ref, weight_ref, True)
    far_back(count, mixed, leaving, cols)
    part = jnp.sum(jnp.sum(arrived[...], axis=0), axis=0, keepdims=True)
    leaving[:, cols:] = jnp.broadcast_to(part[None], (count, leaving.shape[1] - cols, chans))
    exchange_start(count, me, leaving, landed, send_b, recv_b)
    for level, flat in enumerate(flats):
        first = offset(count, level)
        total = max(count >> (level + 1), 1)
        prior = other_ref[first : first + total].astype(F32).reshape(total * cols, chans)
        far[level * tiles : (level + 1) * tiles] = outer(prior.astype(BF16), flat).reshape(
            tiles, 8, chans
        )
    streams[1].start(0)
    for index in range(max(len(stream.stages) for stream in streams)):
        for stream in streams:
            if index < len(stream.stages):
                stream.finish(index)
                stream.start(index + 1)
    exchange_wait(count, me, leaving, landed, send_b, recv_b)
    out_ref[...] = landed[:, 0:cols]
    bias_ref[...] = jnp.sum(landed[:, cols : cols + 8], axis=0) * scale_all
    point = jnp.zeros((chans, chans), F32)
    for level in range(len(scales)):
        source, base = (near_sum, level)
        if level >= first_level:
            source, base = (far_sum, level - first_level)
        raw = source[base * tiles : (base + 1) * tiles].reshape(chans, chans) * scales[level]
        mix_ref[level] = (raw * factors[level]).astype(BF16)
        point = point + raw
    point_ref[...] = (point * scale_all).astype(BF16)


def cross(coarse, weights, first_level):
    count, cols, chans = coarse.shape
    whole = pl.BlockSpec(memory_space=pltpu.VMEM)
    return pl.pallas_call(
        functools.partial(cross_kernel, count, first_level),
        out_shape=(
            jax.ShapeDtypeStruct(coarse.shape, F32),
            jax.ShapeDtypeStruct(coarse.shape, BF16),
        ),
        in_specs=[whole] * 2,
        out_specs=(whole,) * 2,
        scratch_shapes=[pltpu.VMEM(coarse.shape, F32)] * 3 + [pltpu.SemaphoreType.DMA((count,))] * 4,
        compiler_params=pltpu.CompilerParams(
            collective_id=0, has_side_effects=True, vmem_limit_bytes=32 << 20
        ),
    )(coarse, weights)


def cross_back(coarse, weights, other, local, first_level, factors, scales, scale_all):
    count, cols, chans = coarse.shape
    levels = weights.shape[0]
    whole = pl.BlockSpec(memory_space=pltpu.VMEM)
    tiles = chans // 8
    near, far = first_level * tiles, (levels - first_level) * tiles
    depth = count.bit_length() - 1
    padded = (count, cols + 8, chans)
    return pl.pallas_call(
        functools.partial(cross_back_kernel, count, first_level, factors, scales, scale_all),
        out_shape=(
            jax.ShapeDtypeStruct(coarse.shape, F32),
            jax.ShapeDtypeStruct(weights.shape, BF16),
            jax.ShapeDtypeStruct((chans, chans), BF16),
            jax.ShapeDtypeStruct((8, chans), F32),
        ),
        in_specs=[whole] * 4,
        out_specs=(whole,) * 4,
        scratch_shapes=[
            pltpu.VMEM(coarse.shape, BF16),
            pltpu.VMEM(coarse.shape, F32),
            pltpu.VMEM(padded, F32),
            pltpu.VMEM(padded, F32),
            pltpu.VMEM((near, 8, chans), F32),
            pltpu.VMEM((slot_tiles(near, count), 8, chans), F32),
            pltpu.VMEM((near, 8, chans), F32),
            pltpu.VMEM((far, 8, chans), F32),
            pltpu.VMEM((slot_tiles(far, count), 8, chans), F32),
            pltpu.VMEM((far, 8, chans), F32),
        ]
        + [pltpu.SemaphoreType.DMA((count,))] * 4
        + [pltpu.SemaphoreType.DMA((2 * depth,))] * 4,
        compiler_params=pltpu.CompilerParams(
            collective_id=1, has_side_effects=True, vmem_limit_bytes=32 << 20
        ),
    )(coarse, weights, other, local.reshape(near, 8, chans))


def shards(fields, cotangent, point_weight, mix_weight, bias_vec):
    rows, width, chans = fields.shape
    depth = rows.bit_length() - 1
    count = lax.axis_size("gx")
    levels = mix_weight.shape[0]
    step = 32
    blocks = width // step
    scales = [2.0 ** -(level + 1) for level in range(levels - 1)] + [2.0 ** -(levels - 1)]
    scales = np.array(scales, np.float32)
    joined = mix_weight.astype(F32) + point_weight.astype(F32)[None]
    weights = (joined * scales[:, None, None]).astype(BF16)
    bias = jnp.broadcast_to(bias_vec.astype(F32)[None], (8, chans))

    field_spec = pl.BlockSpec((rows, step, chans), lambda i: (0, i, 0))
    coeff_spec = pl.BlockSpec((1, rows, step, chans), lambda i: (i, 0, 0, 0))
    row_spec = pl.BlockSpec((step, chans), lambda i: (i, 0))
    weight_spec = pl.BlockSpec((levels, chans, chans), lambda i: (0, 0, 0))
    grad_spec = pl.BlockSpec((depth, chans, chans), lambda i: (0, 0, 0))
    params = pltpu.CompilerParams(
        dimension_semantics=("arbitrary",), vmem_limit_bytes=48 << 20
    )
    coeff_type = jax.ShapeDtypeStruct((blocks, rows, step, chans), BF16)
    row_type = jax.ShapeDtypeStruct((width, chans), F32)
    mixed_type = pltpu.VMEM((rows, step, chans), F32)

    coeffs, coarse = pl.pallas_call(
        functools.partial(analyse_kernel, depth),
        grid=(blocks,),
        in_specs=[field_spec],
        out_specs=(coeff_spec, row_spec),
        out_shape=(coeff_type, row_type),
        compiler_params=params,
    )(fields)

    far_shape = (count, width // count, chans)
    spectral, far_coeffs = cross(coarse.reshape(far_shape), weights, depth)

    backs, sums, grad_local = pl.pallas_call(
        functools.partial(middle_kernel, depth),
        grid=(blocks,),
        in_specs=[
            coeff_spec, field_spec, row_spec, weight_spec,
            pl.BlockSpec((8, chans), lambda i: (0, 0)),
        ],
        out_specs=(coeff_spec, row_spec, grad_spec),
        out_shape=(coeff_type, row_type, jax.ShapeDtypeStruct((depth, chans, chans), F32)),
        scratch_shapes=[mixed_type],
        compiler_params=params,
    )(coeffs, cotangent, spectral.reshape(width, chans), weights, bias)

    total_rows = rows * count
    members = [width * total_rows / 2 ** (level + 1) for level in range(levels - 1)] + [width]
    factors = [1.0 / math.sqrt(value) for value in members]
    scale_all = 1.0 / math.sqrt(total_rows * width)
    spectral_back, grad_mix, grad_point, grad_bias = cross_back(
        sums.reshape(far_shape), weights, far_coeffs, grad_local, depth,
        factors, [float(value) for value in scales], scale_all,
    )

    (grad_input,) = pl.pallas_call(
        functools.partial(synth_kernel, depth),
        grid=(blocks,),
        in_specs=[coeff_spec, row_spec, weight_spec],
        out_specs=(field_spec,),
        out_shape=(jax.ShapeDtypeStruct(fields.shape, BF16),),
        scratch_shapes=[mixed_type],
        compiler_params=params,
        cost_estimate=pl.CostEstimate(
            flops=2 * rows * width * chans * chans, bytes_accessed=4 * rows * width * chans,
            transcendentals=0,
        ),
    )(backs, spectral_back.reshape(width, chans), weights)

    grad_bias = grad_bias[0].astype(BF16)
    return (grad_input, grad_mix, grad_point, grad_bias)


def solution(mesh):
    in_specs = (P("gx", "ga", None), P("gx", "ga", None), P(), P(), P())
    out_specs = (P("gx", "ga", None), P("ga", None, None), P("ga", None), P("ga"))
    return jax.shard_map(shards, mesh=mesh, in_specs=in_specs, out_specs=out_specs, check_vma=False)
```

time: 178 us -> 98.5 us (0.55)
  waiting for transfers between devices: 80.7 us -> 0 us
  Pallas kernels: 72.6 us -> 92.8 us
  between operations: 14.2 us -> 0.65 us
  local copies, waits for them, and re-layouts: 5.6 us -> 2.53 us
  other arithmetic: 4.04 us -> 1.9 us
    psum x1 -> x0, waiting for transfers between devices: 80.7 us -> none  [shards(): totals = lax.psum(jnp.concatenate([grads, bias_local], axis=0), 'gx')]
    pallas_call x2, Pallas kernels: 30.3 us -> 50.6 us  [the longest x1 34.3 us: cross_back(): pl.pallas_call(functools.partial(cross_back_kernel, count, first_level, f...]
  transfers between devices with their start and end apart: 1 -> 0, of which waited for: 1 -> 0; matrix products, arithmetic and copies ran while one was open for 0% -> 0% of each run, Pallas kernels for 6% -> 0%
where the time goes in v2:
time: 98.5 us; the launch traced here: 97.9 us
  Pallas kernels  92.8 us (94%)
  local copies, waits for them, and re-layouts  2.53 us (3%)
  other arithmetic  1.9 us (2%)
    pallas_call x1, Pallas kernels, cross_back(): pl.pallas_call(functools.partial(cross_back_kernel, count, first_level, f...  34.3 us
    pallas_call x1, Pallas kernels, shards(): pl.pallas_call(functools.partial(middle_kernel, depth), grid=(blocks,), i...  22 us
    pallas_call x1, Pallas kernels, cross(): pl.pallas_call(functools.partial(cross_kernel, count, first_level), out_s...  16.3 us
    pallas_call x1, Pallas kernels, shards(): pl.pallas_call(functools.partial(synth_kernel, depth), grid=(blocks,), in...  10.5 us
    pallas_call x1, Pallas kernels, shards(): pl.pallas_call(functools.partial(analyse_kernel, depth), grid=(blocks,),...  9.64 us

profile of v2, /device:TPU:0, one launch (start us, length us, event | category | flops | bytes accessed | tf_op | source)
XLA Modules:
  0.0 97.9 jit_solution(4832319437475408118)
XLA Ops:
  0.6 0.7 broadcast_in_dim.2.bias_ref
  1.3 0.8 convert_element_type.17
  2.1 1.1 %multiply_convert_fusion.weight_ref = bf16[12,128,128]{2,1,0:T(8,128)(2,1)S(1)} fusion(bf16[12,128,128]{2,1,0:T(8,128)(2,1)} %param.9, f32[12]{0:T(128)} %constant.3, f32[128,128]{1,0:T(8,128)S(1)} %convert_element_type.17), kind=kLoop, calls=%fused_computation | loop fusion | flops 786432 | bytes 852016 | tf_op jit(solution)/shard_map/convert_element_type | solution.py:389
  3.2 9.6 %shard_map.93 = (bf16[8,128,32,128]{3,2,1,0:T(8,128)(2,1)}, f32[256,128]{1,0:T(8,128)S(1)}) custom-call(bf16[128,256,128]{2,1,0:T(8,128)(2,1)} %fields_ref.1), custom_call_target="tpu_custom_call" | custom-call | tf_op jit(solution)/shard_map/pallas_call | solution.py:404
  12.8 16.3 %shard_map.94 = (f32[16,16,128]{2,1,0:T(8,128)S(1)}, bf16[16,16,128]{2,1,0:T(8,128)(2,1)S(1)}) custom-call(f32[16,16,128]{2,1,0:T(8,128)S(1)} %bitcast.10, bf16[12,128,128]{2,1,0:T(8,128)(2,1)S(1)} %multiply_convert_fusion.weight_ref), custom_call_target="tpu_custom_call" | custom-call | tf_op jit(solution)/shard_map/pallas_call | solution.py:326
  29.2 22.0 %shard_map.95 = (bf16[8,128,32,128]{3,2,1,0:T(8,128)(2,1)}, f32[256,128]{1,0:T(8,128)S(1)}, f32[7,128,128]{2,1,0:T(8,128)S(1)}) custom-call(bf16[8,128,32,128]{3,2,1,0:T(8,128)(2,1)} %get-tuple-element.15.coeff_ref, bf16[128,256,128]{2,1,0:T(8,128)(2,1)} %cot_ref.1, f32[256,128]{1,0:T(8,128)S(1)} %bitcast.9, ...), custom_call_target="tpu_custom_call" | custom-call | tf_op jit(solution)/shard_map/pallas_call | solution.py:416
  51.2 34.3 %shard_map.96 = (f32[16,16,128]{2,1,0:T(8,128)S(1)}, bf16[12,128,128]{2,1,0:T(8,128)(2,1)S(1)}, bf16[128,128]{1,0:T(8,128)(2,1)S(1)}, f32[8,128]{1,0:T(8,128)S(1)}) custom-call(f32[16,16,128]{2,1,0:T(8,128)S(1)} %bitcast.11, bf16[12,128,128]{2,1,0:T(8,128)(2,1)S(1)} %multiply_convert_fusion.weight_ref, bf16[16,16,128]{2,1,0:T(8,128)(2,1)S(1)} %get-tuple-element.20.other_ref, ...), custom_call_target="tpu_custom_call" | custom-call | tf_op jit(solution)/shard_map/pallas_call | solution.py:349
  85.5 10.5 %shard_map.97 = bf16[128,256,128]{2,1,0:T(8,128)(2,1)} custom-call(bf16[8,128,32,128]{3,2,1,0:T(8,128)(2,1)} %get-tuple-element.18.back_ref, f32[256,128]{1,0:T(8,128)S(1)} %bitcast.8, bf16[12,128,128]{2,1,0:T(8,128)(2,1)S(1)} %multiply_convert_fusion.weight_ref), custom_call_target="tpu_custom_call" | custom-call | flops 1073741824 | bytes 16777216 | tf_op jit(solution)/shard_map/pallas_call | solution.py:438
  96.0 0.5 slice_bitcast_fusion
  96.5 0.7 copy.12
  97.3 0.6 copy.13
  (1 shorter events, 0.0 us)

commit v3 on v2

v3 whole, which is shorter than its diff:
```python
import functools
import math

import jax
import jax.numpy as jnp
import numpy as np
from jax import lax
from jax.experimental import pallas as pl
from jax.experimental.pallas import tpu as pltpu
from jax.sharding import PartitionSpec as P

F32 = jnp.float32
BF16 = jnp.bfloat16
LANES = 16
GELU_K = math.sqrt(2.0 / math.pi)
GELU_C = 0.044715


def offset(rows, level):
    return rows - (rows >> level)


def outer(left, right):
    return lax.dot_general(left, right, (((0,), (0,)), ((), ())), preferred_element_type=F32)


def apply_weight(rows, weight, turned):
    sides = (((1,), (1 if turned else 0,)), ((), ()))
    return lax.dot_general(rows, weight, sides, preferred_element_type=F32)


def slope_of(value, cot):
    square = value * value
    inner = value * (GELU_K + (GELU_K * GELU_C) * square)
    half = 0.5 + 0.5 * jnp.tanh(inner)
    ramp = value * (2.0 * GELU_K + (6.0 * GELU_K * GELU_C) * square)
    return cot * (half * (1.0 + (1.0 - half) * ramp))


def mix_block(depth, coeff_ref, weight_ref, mixed_ref, turned):
    rows = 1 << depth
    wide = coeff_ref.shape[1]
    for level in range(depth):
        first, count = offset(rows, level), rows >> (level + 1)
        flat = coeff_ref[first : first + count].reshape(count * wide, coeff_ref.shape[2])
        mixed_ref[first : first + count] = apply_weight(flat, weight_ref[level], turned).reshape(
            count, wide, weight_ref.shape[2]
        )


def synth_kernel(depth, back_ref, coarse_ref, weight_ref, out_ref, mixed_ref):
    rows = 1 << depth
    mix_block(depth, back_ref.at[0], weight_ref, mixed_ref, True)

    @pl.loop(0, back_ref.shape[2] // LANES)
    def _(sub):
        cols = pl.ds(pl.multiple_of(sub * LANES, LANES), LANES)

        def tree(level, index, value):
            if level == 0:
                out_ref[index, cols, :] = value.astype(BF16)
                return
            detail = mixed_ref[offset(rows, level - 1) + index, cols, :]
            tree(level - 1, 2 * index, value - detail)
            tree(level - 1, 2 * index + 1, value + detail)

        tree(depth, 0, coarse_ref[cols, :])


class Stream:
    def __init__(self, total, slots, result, send, recv, bits, me):
        self.total, self.slots, self.result = total, slots, result
        self.send, self.recv = send, recv
        start, length, place = 0, total.shape[0], 0
        self.plan = []
        for turn, bit in enumerate(bits):
            upper = lax.rem(me // (1 << bit), 2)
            partner = me + (1 - 2 * upper) * (1 << bit)
            halved = length % 2 == 0
            size = length // 2 if halved else length
            keep = start + upper * size if halved else start
            give = start + (1 - upper) * size if halved else start
            self.plan.append((turn, partner, halved, size, keep, give, place))
            start, length, place = keep, size, place + size
        self.stages = [("sum",) + item for item in self.plan]
        self.stages += [("spread",) + item for item in self.plan[::-1] if item[2]]

    def copy(self, index):
        kind, turn, partner, halved, size, keep, give, place = self.stages[index]
        if kind == "sum":
            source = self.total.at[pl.ds(give, size)]
            target = self.slots.at[pl.ds(place, size)]
        else:
            source = self.result.at[pl.ds(keep, size)]
            target = self.result.at[pl.ds(keep, size)]
        return pltpu.make_async_remote_copy(
            src_ref=source,
            dst_ref=target,
            send_sem=self.send.at[index],
            recv_sem=self.recv.at[index],
            device_id={"gx": partner},
            device_id_type=pl.DeviceIdType.MESH,
        )

    def start(self, index):
        if index < len(self.stages):
            self.copy(index).start()

    def finish(self, index):
        self.copy(index).wait()
        kind, turn, partner, halved, size, keep, give, place = self.stages[index]
        if kind == "sum":
            here = pl.ds(keep, size)
            into = self.result if turn == len(self.plan) - 1 else self.total
            into[here] = self.total[here] + self.slots[pl.ds(place, size)]


def slot_tiles(tiles, count):
    used = 0
    for _ in range(count.bit_length() - 1):
        tiles = tiles // 2 if tiles % 2 == 0 else tiles
        used += tiles
    return used


def far_levels(count, first_level, arrived, coeff_ref, weight_ref, turned):
    depth = count.bit_length() - 1
    cols, chans = arrived.shape[1], arrived.shape[2]

    def down(level, index):
        if level == 0:
            return arrived[index]
        even = down(level - 1, 2 * index)
        odd = down(level - 1, 2 * index + 1)
        coeff_ref[offset(count, level - 1) + index] = (odd - even).astype(BF16)
        return even + odd

    coeff_ref[count - 1] = down(depth, 0).astype(BF16)
    mixed, flats = [], []
    for level in range(depth + 1):
        first = offset(count, level)
        total = max(count >> (level + 1), 1)
        flat = coeff_ref[first : first + total].astype(F32).reshape(total * cols, chans).astype(BF16)
        flats.append(flat)
        mixed.append(
            apply_weight(flat, weight_ref[first_level + level], turned).reshape(total, cols, chans)
        )
    return mixed, flats


def far_back(count, mixed, leaving, cols):
    depth = count.bit_length() - 1

    def up(level, index, value):
        if level == 0:
            leaving[index, 0:cols] = value
            return
        detail = mixed[level - 1][index]
        up(level - 1, 2 * index, value - detail)
        up(level - 1, 2 * index + 1, value + detail)

    up(depth, 0, mixed[depth][0])


def swap(count, me, source, target, send, recv, step):
    peer = lax.rem(me + step, count)
    return pltpu.make_async_remote_copy(
        src_ref=source.at[peer],
        dst_ref=target.at[me],
        send_sem=send.at[step],
        recv_sem=recv.at[step],
        device_id={"gx": peer},
        device_id_type=pl.DeviceIdType.MESH,
    )


def exchange_start(count, me, source, target, send, recv):
    @pl.loop(1, count)
    def _(step):
        swap(count, me, source, target, send, recv, step).start()

    target[me] = source[me]


def exchange_wait(count, me, source, target, send, recv):
    @pl.loop(1, count)
    def _(step):
        swap(count, me, source, target, send, recv, step).wait()


def send_block(count, me, block, share, source, target, send, recv):
    @pl.loop(0, share)
    def _(turn):
        step = lax.rem(block * share + turn - me + count, count)

        @pl.when(step > 0)
        def _():
            swap(count, me, source, target, send, recv, step).start()


def main_kernel(
    count, depth, factors, scales, scale_all,
    fields_ref, cot_ref, weight_ref, bias_ref,
    back_ref, out_ref, mix_ref, point_ref, gbias_ref,
    coeff, mixed_all, far_coeff, far_scratch,
    source_a, arrived_a, leaving_a, landed_a,
    source_b, arrived_b, leaving_b, landed_b,
    near, near_slots, near_sum, far, far_slots, far_sum,
    send_a, recv_a, send_b, recv_b, send_c, recv_c, send_d, recv_d,
    send_n, recv_n, send_f, recv_f,
):
    me = lax.axis_index("gx")
    turn = pl.program_id(0)
    blocks, rows, wide, chans = coeff.shape
    cols = source_a.shape[1]
    tiles = chans // 8
    share, piece = wide // cols, LANES // cols
    bits = list(range(count.bit_length() - 1))
    barrier = pltpu.get_barrier_semaphore()

    @pl.when(turn == 0)
    def _():
        @pl.loop(1, count)
        def _(step):
            pl.semaphore_signal(
                barrier,
                inc=1,
                device_id={"gx": lax.rem(me + step, count)},
                device_id_type=pl.DeviceIdType.MESH,
            )

        near[...] = jnp.zeros_like(near)

    @pl.when(turn < blocks)
    def _():
        @pl.loop(0, wide // LANES)
        def _(sub):
            here = pl.ds(pl.multiple_of(sub * LANES, LANES), LANES)

            def tree(level, index):
                if level == 0:
                    return fields_ref[index, here, :].astype(F32)
                even = tree(level - 1, 2 * index)
                odd = tree(level - 1, 2 * index + 1)
                coeff[turn, offset(rows, level - 1) + index, here, :] = (odd - even).astype(BF16)
                return even + odd

            source_a[pl.ds(turn * share + sub * piece, piece)] = tree(depth, 0).reshape(
                piece, cols, chans
            )

        @pl.when(turn == 0)
        def _():
            pl.semaphore_wait(barrier, count - 1)

        send_block(count, me, turn, share, source_a, arrived_a, send_a, recv_a)

    @pl.when(turn == blocks)
    def _():
        @pl.loop(0, blocks // 2)
        def _(block):
            mix_block(depth, coeff.at[block], weight_ref, mixed_all.at[block], False)

        arrived_a[me] = source_a[me]
        exchange_wait(count, me, source_a, arrived_a, send_a, recv_a)
        mixed, _ = far_levels(count, depth, arrived_a, far_coeff, weight_ref, False)
        far_back(count, mixed, leaving_a, cols)
        exchange_start(count, me, leaving_a, landed_a, send_b, recv_b)

        @pl.loop(blocks // 2, blocks)
        def _(block):
            mix_block(depth, coeff.at[block], weight_ref, mixed_all.at[block], False)

        exchange_wait(count, me, leaving_a, landed_a, send_b, recv_b)

    @pl.when(turn >= blocks)
    def _():
        block = turn - blocks

        @pl.loop(0, wide // LANES)
        def _(sub):
            here = pl.ds(pl.multiple_of(sub * LANES, LANES), LANES)

            def tree(level, index, value):
                if level == 0:
                    cot = cot_ref[index, here, :].astype(F32)
                    return slope_of(value, cot).astype(BF16).astype(F32)
                place = offset(rows, level - 1) + index
                detail = mixed_all[block, place, here, :]
                even = tree(level - 1, 2 * index, value - detail)
                odd = tree(level - 1, 2 * index + 1, value + detail)
                back_ref[0, place, here, :] = (odd - even).astype(BF16)
                return even + odd

            pieces = pl.ds(block * share + sub * piece, piece)
            start = landed_a[pieces].reshape(LANES, chans) + bias_ref[0:1, :]
            source_b[pieces] = tree(depth, 0, start).reshape(piece, cols, chans)

        send_block(count, me, block, share, source_b, arrived_b, send_c, recv_c)
        for level in range(depth):
            first, number = offset(rows, level), rows >> (level + 1)
            left = coeff[block, first : first + number].reshape(number * wide, chans)
            right = back_ref[0, first : first + number].reshape(number * wide, chans)
            near[level * tiles : (level + 1) * tiles] += outer(left, right).reshape(tiles, 8, chans)

    @pl.when(turn == 2 * blocks - 1)
    def _():
        streams = [Stream(near, near_slots, near_sum, send_n, recv_n, bits, me)]
        other = bits[:1] + bits[2:] + bits[1:2]
        streams.append(Stream(far, far_slots, far_sum, send_f, recv_f, other, me))
        streams[0].start(0)
        arrived_b[me] = source_b[me]
        exchange_wait(count, me, source_b, arrived_b, send_c, recv_c)
        mixed, flats = far_levels(count, depth, arrived_b, far_scratch, weight_ref, True)
        far_back(count, mixed, leaving_b, cols)
        part = jnp.sum(jnp.sum(arrived_b[...], axis=0), axis=0, keepdims=True)
        leaving_b[:, cols:] = jnp.broadcast_to(part[None], (count, leaving_b.shape[1] - cols, chans))
        exchange_start(count, me, leaving_b, landed_b, send_d, recv_d)
        for level, flat in enumerate(flats):
            first = offset(count, level)
            total = max(count >> (level + 1), 1)
            prior = far_coeff[first : first + total].astype(F32).reshape(total * cols, chans)
            far[level * tiles : (level + 1) * tiles] = outer(prior.astype(BF16), flat).reshape(
                tiles, 8, chans
            )
        streams[1].start(0)
        for index in range(max(len(stream.stages) for stream in streams)):
            for stream in streams:
                if index < len(stream.stages):
                    stream.finish(index)
                    stream.start(index + 1)
        exchange_wait(count, me, leaving_b, landed_b, send_d, recv_d)
        out_ref[...] = landed_b[:, 0:cols]
        gbias_ref[...] = jnp.sum(landed_b[:, cols : cols + 8], axis=0) * scale_all
        point = jnp.zeros((chans, chans), F32)
        for level in range(len(scales)):
            source, base = (near_sum, level) if level < depth else (far_sum, level - depth)
            raw = source[base * tiles : (base + 1) * tiles].reshape(chans, chans) * scales[level]
            mix_ref[level] = (raw * factors[level]).astype(BF16)
            point = point + raw
        point_ref[...] = (point * scale_all).astype(BF16)


def main_call(fields, cotangent, weights, bias, step, count, factors, scales, scale_all):
    rows, width, chans = fields.shape
    depth = rows.bit_length() - 1
    levels = weights.shape[0]
    blocks, cols = width // step, width // count
    tiles = chans // 8
    near, far = depth * tiles, (levels - depth) * tiles
    turns = count.bit_length() - 1
    row_shape, padded = (count, cols, chans), (count, cols + 8, chans)
    whole = lambda shape: pl.BlockSpec(shape, lambda i: (0,) * len(shape))
    rows_f32 = pltpu.VMEM(row_shape, F32)
    return pl.pallas_call(
        functools.partial(main_kernel, count, depth, factors, scales, scale_all),
        grid=(2 * blocks,),
        in_specs=[
            pl.BlockSpec((rows, step, chans), lambda i: (0, jnp.minimum(i, blocks - 1), 0)),
            pl.BlockSpec((rows, step, chans), lambda i: (0, jnp.maximum(i - blocks, 0), 0)),
            whole(weights.shape),
            whole(bias.shape),
        ],
        out_specs=(
            pl.BlockSpec((1, rows, step, chans), lambda i: (jnp.maximum(i - blocks, 0), 0, 0, 0)),
            whole(row_shape),
            whole(weights.shape),
            whole((chans, chans)),
            whole((8, chans)),
        ),
        out_shape=(
            jax.ShapeDtypeStruct((blocks, rows, step, chans), BF16),
            jax.ShapeDtypeStruct(row_shape, F32),
            jax.ShapeDtypeStruct(weights.shape, BF16),
            jax.ShapeDtypeStruct((chans, chans), BF16),
            jax.ShapeDtypeStruct((8, chans), F32),
        ),
        scratch_shapes=[
            pltpu.VMEM((blocks, rows, step, chans), BF16),
            pltpu.VMEM((blocks, rows, step, chans), F32),
            pltpu.VMEM(row_shape, BF16),
            pltpu.VMEM(row_shape, BF16),
            rows_f32, rows_f32, rows_f32, rows_f32,
            rows_f32, rows_f32, pltpu.VMEM(padded, F32), pltpu.VMEM(padded, F32),
            pltpu.VMEM((near, 8, chans), F32),
            pltpu.VMEM((slot_tiles(near, count), 8, chans), F32),
            pltpu.VMEM((near, 8, chans), F32),
            pltpu.VMEM((far, 8, chans), F32),
            pltpu.VMEM((slot_tiles(far, count), 8, chans), F32),
            pltpu.VMEM((far, 8, chans), F32),
        ]
        + [pltpu.SemaphoreType.DMA((count,))] * 8
        + [pltpu.SemaphoreType.DMA((2 * turns,))] * 4,
        compiler_params=pltpu.CompilerParams(
            dimension_semantics=("arbitrary",), collective_id=0, has_side_effects=True,
            vmem_limit_bytes=56 << 20,
        ),
    )(fields, cotangent, weights, bias)


def shards(fields, cotangent, point_weight, mix_weight, bias_vec):
    rows, width, chans = fields.shape
    depth = rows.bit_length() - 1
    count = lax.axis_size("gx")
    levels = mix_weight.shape[0]
    step = 32
    blocks = width // step
    scales = [2.0 ** -(level + 1) for level in range(levels - 1)] + [2.0 ** -(levels - 1)]
    scales = np.array(scales, np.float32)
    joined = mix_weight.astype(F32) + point_weight.astype(F32)[None]
    weights = (joined * scales[:, None, None]).astype(BF16)
    bias = jnp.broadcast_to(bias_vec.astype(F32)[None], (8, chans))

    field_spec = pl.BlockSpec((rows, step, chans), lambda i: (0, i, 0))
    coeff_spec = pl.BlockSpec((1, rows, step, chans), lambda i: (i, 0, 0, 0))
    row_spec = pl.BlockSpec((step, chans), lambda i: (i, 0))
    weight_spec = pl.BlockSpec((levels, chans, chans), lambda i: (0, 0, 0))
    params = pltpu.CompilerParams(
        dimension_semantics=("arbitrary",), vmem_limit_bytes=48 << 20
    )
    mixed_type = pltpu.VMEM((rows, step, chans), F32)

    total_rows = rows * count
    members = [width * total_rows / 2 ** (level + 1) for level in range(levels - 1)] + [width]
    factors = [1.0 / math.sqrt(value) for value in members]
    scale_all = 1.0 / math.sqrt(total_rows * width)
    backs, spectral_back, grad_mix, grad_point, grad_bias = main_call(
        fields, cotangent, weights, bias, step, count,
        factors, [float(value) for value in scales], scale_all,
    )

    (grad_input,) = pl.pallas_call(
        functools.partial(synth_kernel, depth),
        grid=(blocks,),
        in_specs=[coeff_spec, row_spec, weight_spec],
        out_specs=(field_spec,),
        out_shape=(jax.ShapeDtypeStruct(fields.shape, BF16),),
        scratch_shapes=[mixed_type],
        compiler_params=params,
        cost_estimate=pl.CostEstimate(
            flops=2 * rows * width * chans * chans, bytes_accessed=4 * rows * width * chans,
            transcendentals=0,
        ),
    )(backs, spectral_back.reshape(width, chans), weights)

    grad_bias = grad_bias[0].astype(BF16)
    return (grad_input, grad_mix, grad_point, grad_bias)


def solution(mesh):
    in_specs = (P("gx", "ga", None), P("gx", "ga", None), P(), P(), P())
    out_specs = (P("gx", "ga", None), P("ga", None, None), P("ga", None), P("ga"))
    return jax.shard_map(shards, mesh=mesh, in_specs=in_specs, out_specs=out_specs, check_vma=False)
```

time: 98.5 us -> 87.1 us (0.88)
  Pallas kernels: 92.8 us -> 79.2 us
  local copies, waits for them, and re-layouts: 2.53 us -> 4.04 us
    pallas_call x4 -> x1, Pallas kernels: 82.3 us -> 68.6 us  [main_call(): pl.pallas_call(functools.partial(main_kernel, count, depth, factors, scal...]
    unnamed x2 -> x12, local copies, waits for them, and re-layouts: 1.36 us -> 2.27 us
where the time goes in v3:
time: 87.1 us; the launch traced here: 86.5 us
  Pallas kernels  79.2 us (91%)
  local copies, waits for them, and re-layouts  4.04 us (5%)
  other arithmetic  2.64 us (3%)
    pallas_call x1, Pallas kernels, main_call(): pl.pallas_call(functools.partial(main_kernel, count, depth, factors, scal...  68.6 us
    pallas_call x1, Pallas kernels, shards(): pl.pallas_call(functools.partial(synth_kernel, depth), grid=(blocks,), in...  10.6 us
    unnamed x12, local copies, waits for them, and re-layouts  2.27 us
    convert_element_type x1, other arithmetic, shards(): weights = (joined * scales[:, None, None]).astype(BF16)  1.88 us

profile of v3, /device:TPU:0, one launch (start us, length us, event | category | flops | bytes accessed | tf_op | source)
XLA Modules:
  0.0 86.5 jit_solution(10474146465973756893)
XLA Ops:
  0.6 1.2 %broadcast_in_dim.2.bias_ref = f32[8,128]{1,0:T(8,128)} broadcast(bf16[128]{0:T(256)(128)(2,1)} %param.10), dimensions={1} | broadcast | bytes 4352 | tf_op jit(solution)/shard_map/broadcast_in_dim | solution.py:412
  1.9 0.8 convert_element_type.17
  2.6 1.9 %multiply_convert_fusion.weight_ref = bf16[12,128,128]{2,1,0:T(8,128)(2,1)} fusion(bf16[12,128,128]{2,1,0:T(8,128)(2,1)} %param.9, f32[12]{0:T(128)} %constant.3, f32[128,128]{1,0:T(8,128)S(1)} %convert_element_type.17), kind=kLoop, calls=%fused_computation | loop fusion | flops 786432 | bytes 852016 | tf_op jit(solution)/shard_map/convert_element_type | solution.py:411
  4.5 0.0 copy-start
  4.5 68.6 %shard_map.93 = (bf16[8,128,32,128]{3,2,1,0:T(8,128)(2,1)}, f32[16,16,128]{2,1,0:T(8,128)}, bf16[12,128,128]{2,1,0:T(8,128)(2,1)}, bf16[128,128]{1,0:T(8,128)(2,1)}, f32[8,128]{1,0:T(8,128)}) custom-call(bf16[128,256,128]{2,1,0:T(8,128)(2,1)} %fields_ref.1, bf16[128,256,128]{2,1,0:T(8,128)(2,1)} %cot_ref.1, ...), custom_call_target="tpu_custom_call" | custom-call | tf_op jit(solution)/shard_map/pallas_call | solution.py:355
  73.1 0.0 copy-done
  73.2 0.0 copy-start.1
  73.2 0.9 %copy-done.1 = f32[16,16,128]{2,1,0:T(8,128)S(1)} copy-done((f32[16,16,128]{2,1,0:T(8,128)S(1)}, f32[16,16,128]{2,1,0:T(8,128)}, u32[]{:S(2)}) %copy-start.1) | copy-done | bytes 131096
  74.1 0.0 copy-start.4
  74.1 0.0 copy-start.2
  74.1 0.0 copy-start.3
  74.1 10.6 %shard_map.94 = bf16[128,256,128]{2,1,0:T(8,128)(2,1)} custom-call(bf16[8,128,32,128]{3,2,1,0:T(8,128)(2,1)} %get-tuple-element.9.back_ref, f32[256,128]{1,0:T(8,128)S(1)} %bitcast.3, bf16[12,128,128]{2,1,0:T(8,128)(2,1)S(1)} %copy-done), custom_call_target="tpu_custom_call" | custom-call | flops 1073741824 | bytes 16777216 | tf_op jit(solution)/shard_map/pallas_call | solution.py:432
  84.6 0.0 copy-done.4
  84.6 0.5 slice_bitcast_fusion
  85.2 0.0 copy-done.2
  85.2 0.7 copy.12
  85.9 0.0 copy-done.3
  85.9 0.6 copy.13
  (1 shorter events, 0.0 us)
Async XLA Ops:
  4.5 68.6 %copy-start = (bf16[12,128,128]{2,1,0:T(8,128)(2,1)S(1)}, bf16[12,128,128]{2,1,0:T(8,128)(2,1)}, u32[]{:S(2)}) copy-start(bf16[12,128,128]{2,1,0:T(8,128)(2,1)} %multiply_convert_fusion.weight_ref) | copy-start | bytes 1179652
  73.2 0.9 %copy-start.1 = (f32[16,16,128]{2,1,0:T(8,128)S(1)}, f32[16,16,128]{2,1,0:T(8,128)}, u32[]{:S(2)}) copy-start(f32[16,16,128]{2,1,0:T(8,128)} %get-tuple-element.10) | copy-start | bytes 393220
  74.1 10.6 %copy-start.4 = (f32[8,128]{1,0:T(8,128)S(1)}, f32[8,128]{1,0:T(8,128)}, u32[]{:S(2)}) copy-start(f32[8,128]{1,0:T(8,128)} %get-tuple-element.13) | copy-start | bytes 12292
  74.1 11.1 %copy-start.2 = (bf16[12,128,128]{2,1,0:T(8,128)(2,1)S(1)}, bf16[12,128,128]{2,1,0:T(8,128)(2,1)}, u32[]{:S(2)}) copy-start(bf16[12,128,128]{2,1,0:T(8,128)(2,1)} %get-tuple-element.19) | copy-start | bytes 1179652
  74.1 11.8 %copy-start.3 = (bf16[128,128]{1,0:T(8,128)(2,1)S(1)}, bf16[128,128]{1,0:T(8,128)(2,1)}, u32[]{:S(2)}) copy-start(bf16[128,128]{1,0:T(8,128)(2,1)} %get-tuple-element.20) | copy-start | bytes 98308

commit v4 on v3

--- a/solution.py
+++ b/solution.py
@@ -3,7 +3,6 @@
 
 import jax
 import jax.numpy as jnp
-import numpy as np
 from jax import lax
 from jax.experimental import pallas as pl
 from jax.experimental.pallas import tpu as pltpu
@@ -35,6 +34,12 @@
     half = 0.5 + 0.5 * jnp.tanh(inner)
     ramp = value * (2.0 * GELU_K + (6.0 * GELU_K * GELU_C) * square)
     return cot * (half * (1.0 + (1.0 - half) * ramp))
+
+
+def join_weights(mix_ref, point_ref, scales, joined):
+    point = point_ref[...].astype(F32)
+    for level, scale in enumerate(scales):
+        joined[level] = ((mix_ref[level].astype(F32) + point) * scale).astype(BF16)
 
 
 def mix_block(depth, coeff_ref, weight_ref, mixed_ref, turned):
@@ -48,8 +53,15 @@
         )
 
 
-def synth_kernel(depth, back_ref, coarse_ref, weight_ref, out_ref, mixed_ref):
+def synth_kernel(
+    depth, scales, back_ref, coarse_ref, raw_mix_ref, raw_point_ref, out_ref, mixed_ref, weight_ref
+):
     rows = 1 << depth
+
+    @pl.when(pl.program_id(0) == 0)
+    def _():
+        join_weights(raw_mix_ref, raw_point_ref, scales, weight_ref)
+
     mix_block(depth, back_ref.at[0], weight_ref, mixed_ref, True)
 
     @pl.loop(0, back_ref.shape[2] // LANES)
@@ -200,9 +212,9 @@
 
 def main_kernel(
     count, depth, factors, scales, scale_all,
-    fields_ref, cot_ref, weight_ref, bias_ref,
+    fields_ref, cot_ref, raw_mix_ref, raw_point_ref, bias_ref,
     back_ref, out_ref, mix_ref, point_ref, gbias_ref,
-    coeff, mixed_all, far_coeff, far_scratch,
+    weight_ref, coeff, mixed_all, far_coeff, far_scratch,
     source_a, arrived_a, leaving_a, landed_a,
     source_b, arrived_b, leaving_b, landed_b,
     near, near_slots, near_sum, far, far_slots, far_sum,
@@ -230,6 +242,7 @@
             )
 
         near[...] = jnp.zeros_like(near)
+        join_weights(raw_mix_ref, raw_point_ref, scales, weight_ref)
 
     @pl.when(turn < blocks)
     def _():
@@ -293,7 +306,7 @@
                 return even + odd
 
             pieces = pl.ds(block * share + sub * piece, piece)
-            start = landed_a[pieces].reshape(LANES, chans) + bias_ref[0:1, :]
+            start = landed_a[pieces].reshape(LANES, chans) + bias_ref[...].astype(F32)
             source_b[pieces] = tree(depth, 0, start).reshape(piece, cols, chans)
 
         send_block(count, me, block, share, source_b, arrived_b, send_c, recv_c)
@@ -310,6 +323,8 @@
         streams.append(Stream(far, far_slots, far_sum, send_f, recv_f, other, me))
         streams[0].start(0)
         arrived_b[me] = source_b[me]
+        streams[0].finish(0)
+        streams[0].start(1)
         exchange_wait(count, me, source_b, arrived_b, send_c, recv_c)
         mixed, flats = far_levels(count, depth, arrived_b, far_scratch, weight_ref, True)
         far_back(count, mixed, leaving_b, cols)
@@ -325,10 +340,10 @@
             )
         streams[1].start(0)
         for index in range(max(len(stream.stages) for stream in streams)):
-            for stream in streams:
-                if index < len(stream.stages):
-                    stream.finish(index)
-                    stream.start(index + 1)
+            for stream, stage in ((streams[1], index), (streams[0], index + 1)):
+                if stage < len(stream.stages):
+                    stream.finish(stage)
+                    stream.start(stage + 1)
         exchange_wait(count, me, leaving_b, landed_b, send_d, recv_d)
         out_ref[...] = landed_b[:, 0:cols]
         gbias_ref[...] = jnp.sum(landed_b[:, cols : cols + 8], axis=0) * scale_all
@@ -341,7 +356,7 @@
         point_ref[...] = (point * scale_all).astype(BF16)
 
 
-def main_call(fields, cotangent, weights, bias, step, count, factors, scales, scale_all):
+def main_call(fields, cotangent, weights, point_weight, bias, step, count, factors, scales, scale_all):
     rows, width, chans = fields.shape
     depth = rows.bit_length() - 1
     levels = weights.shape[0]
@@ -359,6 +374,7 @@
             pl.BlockSpec((rows, step, chans), lambda i: (0, jnp.minimum(i, blocks - 1), 0)),
             pl.BlockSpec((rows, step, chans), lambda i: (0, jnp.maximum(i - blocks, 0), 0)),
             whole(weights.shape),
+            whole(point_weight.shape),
             whole(bias.shape),
         ],
         out_specs=(
@@ -376,6 +392,7 @@
             jax.ShapeDtypeStruct((8, chans), F32),
         ),
         scratch_shapes=[
+            pltpu.VMEM(weights.shape, BF16),
             pltpu.VMEM((blocks, rows, step, chans), BF16),
             pltpu.VMEM((blocks, rows, step, chans), F32),
             pltpu.VMEM(row_shape, BF16),
@@ -395,7 +412,7 @@
             dimension_semantics=("arbitrary",), collective_id=0, has_side_effects=True,
             vmem_limit_bytes=56 << 20,
         ),
-    )(fields, cotangent, weights, bias)
+    )(fields, cotangent, weights, point_weight, bias)
 
 
 def shards(fields, cotangent, point_weight, mix_weight, bias_vec):
@@ -406,10 +423,7 @@
     step = 32
     blocks = width // step
     scales = [2.0 ** -(level + 1) for level in range(levels - 1)] + [2.0 ** -(levels - 1)]
-    scales = np.array(scales, np.float32)
-    joined = mix_weight.astype(F32) + point_weight.astype(F32)[None]
-    weights = (joined * scales[:, None, None]).astype(BF16)
-    bias = jnp.broadcast_to(bias_vec.astype(F32)[None], (8, chans))
+    bias = bias_vec.reshape(1, chans)
 
     field_spec = pl.BlockSpec((rows, step, chans), lambda i: (0, i, 0))
     coeff_spec = pl.BlockSpec((1, rows, step, chans), lambda i: (i, 0, 0, 0))
@@ -425,23 +439,25 @@
     factors = [1.0 / math.sqrt(value) for value in members]
     scale_all = 1.0 / math.sqrt(total_rows * width)
     backs, spectral_back, grad_mix, grad_point, grad_bias = main_call(
-        fields, cotangent, weights, bias, step, count,
-        factors, [float(value) for value in scales], scale_all,
+        fields, cotangent, mix_weight, point_weight, bias, step, count, factors, scales, scale_all,
     )
 
     (grad_input,) = pl.pallas_call(
-        functools.partial(synth_kernel, depth),
+        functools.partial(synth_kernel, depth, scales),
         grid=(blocks,),
-        in_specs=[coeff_spec, row_spec, weight_spec],
+        in_specs=[
+            coeff_spec, row_spec, weight_spec,
+            pl.BlockSpec(point_weight.shape, lambda i: (0, 0)),
+        ],
         out_specs=(field_spec,),
         out_shape=(jax.ShapeDtypeStruct(fields.shape, BF16),),
-        scratch_shapes=[mixed_type],
+        scratch_shapes=[mixed_type, pltpu.VMEM(mix_weight.shape, BF16)],
         compiler_params=params,
         cost_estimate=pl.CostEstimate(
             flops=2 * rows * width * chans * chans, bytes_accessed=4 * rows * width * chans,
             transcendentals=0,
         ),
-    )(backs, spectral_back.reshape(width, chans), weights)
+    )(backs, spectral_back.reshape(width, chans), mix_weight, point_weight)
 
     grad_bias = grad_bias[0].astype(BF16)
     return (grad_input, grad_mix, grad_point, grad_bias)

time: 87.1 us -> 83 us (0.953)
  other arithmetic: 2.64 us -> 0.01 us
  local copies, waits for them, and re-layouts: 4.04 us -> 2.79 us
    convert_element_type x2 -> x0, other arithmetic: 2.64 us -> none  [the longest x1 1.88 us: shards(): weights = (joined * scales[:, None, None]).astype(BF16)]
    broadcast_in_dim x1 -> x0, local copies, waits for them, and re-layouts: 1.25 us -> none  [shards(): bias = jnp.broadcast_to(bias_vec.astype(F32)[None], (8, chans))]
    unnamed x12 -> x14, local copies, waits for them, and re-layouts: 2.27 us -> 2.28 us
where the time goes in v4:
time: 83 us; the launch traced here: 82.5 us
  Pallas kernels  79 us (95%)
  local copies, waits for them, and re-layouts  2.79 us (3%)
    pallas_call x1, Pallas kernels, main_call(): pl.pallas_call(functools.partial(main_kernel, count, depth, factors, scal...  68.4 us
    pallas_call x1, Pallas kernels, shards(): pl.pallas_call(functools.partial(synth_kernel, depth, scales), grid=(bloc...  10.6 us
    unnamed x14, local copies, waits for them, and re-layouts  2.28 us

profile of v4, /device:TPU:0, one launch (start us, length us, event | category | flops | bytes accessed | tf_op | source)
XLA Modules:
  0.0 82.5 jit_solution(11561036281080000889)
XLA Ops:
  0.6 0.0 copy-start
  0.6 0.0 copy-start.2
  0.7 68.4 %shard_map.84 = (bf16[8,128,32,128]{3,2,1,0:T(8,128)(2,1)}, f32[16,16,128]{2,1,0:T(8,128)}, bf16[12,128,128]{2,1,0:T(8,128)(2,1)}, bf16[128,128]{1,0:T(8,128)(2,1)}, f32[8,128]{1,0:T(8,128)}) custom-call(bf16[128,256,128]{2,1,0:T(8,128)(2,1)} %fields_ref.1, bf16[128,256,128]{2,1,0:T(8,128)(2,1)} %cot_ref.1, bf16[12,128,128]{2,1,0:T(8,128)(2,1)} %raw_mix_ref.3, ...), custom_call_target="tpu_custom_call" | custom-call | tf_op jit(solution)/shard_map/pallas_call | solution.py:370
  69.1 0.0 copy-done
  69.1 0.0 copy-done.2
  69.1 0.0 copy-start.1
  69.1 0.9 %copy-done.1 = f32[16,16,128]{2,1,0:T(8,128)S(1)} copy-done((f32[16,16,128]{2,1,0:T(8,128)S(1)}, f32[16,16,128]{2,1,0:T(8,128)}, u32[]{:S(2)}) %copy-start.1) | copy-done | bytes 131096
  70.0 0.0 copy-start.5
  70.0 0.0 copy-start.3
  70.0 0.0 copy-start.4
  70.0 10.6 %shard_map.85 = bf16[128,256,128]{2,1,0:T(8,128)(2,1)} custom-call(bf16[8,128,32,128]{3,2,1,0:T(8,128)(2,1)} %get-tuple-element.9.back_ref, f32[256,128]{1,0:T(8,128)S(1)} %bitcast.4, bf16[12,128,128]{2,1,0:T(8,128)(2,1)S(1)} %copy-done, bf16[128,128]{1,0:T(8,128)(2,1)S(1)} %copy-done.2), custom_call_target="tpu_custom_call" | custom-call | flops 1073741824 | bytes 16777216 | tf_op jit(solution)/shard_map/pallas_call | solution.py:445
  80.6 0.0 copy-done.5
  80.6 0.5 slice_bitcast_fusion
  81.1 0.0 copy-done.3
  81.1 0.7 copy.11
  81.9 0.0 copy-done.4
  81.9 0.6 copy.12
  (1 shorter events, 0.0 us)
Async XLA Ops:
  0.6 68.5 %copy-start = (bf16[12,128,128]{2,1,0:T(8,128)(2,1)S(1)}, bf16[12,128,128]{2,1,0:T(8,128)(2,1)}, u32[]{:S(2)}) copy-start(bf16[12,128,128]{2,1,0:T(8,128)(2,1)} %raw_mix_ref.3) | copy-start | bytes 1179652
  0.6 68.5 %copy-start.2 = (bf16[128,128]{1,0:T(8,128)(2,1)S(1)}, bf16[128,128]{1,0:T(8,128)(2,1)}, u32[]{:S(2)}) copy-start(bf16[128,128]{1,0:T(8,128)(2,1)} %raw_point_ref.3) | copy-start | bytes 98308
  69.1 0.9 %copy-start.1 = (f32[16,16,128]{2,1,0:T(8,128)S(1)}, f32[16,16,128]{2,1,0:T(8,128)}, u32[]{:S(2)}) copy-start(f32[16,16,128]{2,1,0:T(8,128)} %get-tuple-element.10) | copy-start | bytes 393220
  70.0 10.6 %copy-start.5 = (f32[8,128]{1,0:T(8,128)S(1)}, f32[8,128]{1,0:T(8,128)}, u32[]{:S(2)}) copy-start(f32[8,128]{1,0:T(8,128)} %get-tuple-element.13) | copy-start | bytes 12292
  70.0 11.1 %copy-start.3 = (bf16[12,128,128]{2,1,0:T(8,128)(2,1)S(1)}, bf16[12,128,128]{2,1,0:T(8,128)(2,1)}, u32[]{:S(2)}) copy-start(bf16[12,128,128]{2,1,0:T(8,128)(2,1)} %get-tuple-element.19) | copy-start | bytes 1179652
  70.0 11.9 %copy-start.4 = (bf16[128,128]{1,0:T(8,128)(2,1)S(1)}, bf16[128,128]{1,0:T(8,128)(2,1)}, u32[]{:S(2)}) copy-start(bf16[128,128]{1,0:T(8,128)(2,1)} %get-tuple-element.20) | copy-start | bytes 98308

commit v5 on v4

--- a/solution.py
+++ b/solution.py
@@ -420,7 +420,7 @@
     depth = rows.bit_length() - 1
     count = lax.axis_size("gx")
     levels = mix_weight.shape[0]
-    step = 32
+    step = 64
     blocks = width // step
     scales = [2.0 ** -(level + 1) for level in range(levels - 1)] + [2.0 ** -(levels - 1)]
     bias = bias_vec.reshape(1, chans)

time: 83 us -> 79.5 us (0.958)
  Pallas kernels: 79 us -> 75.8 us
    pallas_call x1, Pallas kernels: 68.4 us -> 66.4 us  [main_call(): pl.pallas_call(functools.partial(main_kernel, count, depth, factors, scal...]
    pallas_call x1, Pallas kernels: 10.6 us -> 9.37 us  [shards(): pl.pallas_call(functools.partial(synth_kernel, depth, scales), grid=(bloc...]
where the time goes in v5:
time: 79.5 us; the launch traced here: 79.3 us
  Pallas kernels  75.8 us (95%)
  local copies, waits for them, and re-layouts  2.79 us (4%)
    pallas_call x1, Pallas kernels, main_call(): pl.pallas_call(functools.partial(main_kernel, count, depth, factors, scal...  66.4 us
    pallas_call x1, Pallas kernels, shards(): pl.pallas_call(functools.partial(synth_kernel, depth, scales), grid=(bloc...  9.37 us
    unnamed x14, local copies, waits for them, and re-layouts  2.28 us

profile of v5, /device:TPU:0, one launch (start us, length us, event | category | flops | bytes accessed | tf_op | source)
XLA Modules:
  0.0 79.3 jit_solution(3731107176632406246)
XLA Ops:
  0.6 0.0 copy-start
  0.6 0.0 copy-start.2
  0.7 66.4 %shard_map.84 = (bf16[4,128,64,128]{3,2,1,0:T(8,128)(2,1)}, f32[16,16,128]{2,1,0:T(8,128)}, bf16[12,128,128]{2,1,0:T(8,128)(2,1)}, bf16[128,128]{1,0:T(8,128)(2,1)}, f32[8,128]{1,0:T(8,128)}) custom-call(bf16[128,256,128]{2,1,0:T(8,128)(2,1)} %fields_ref.1, bf16[128,256,128]{2,1,0:T(8,128)(2,1)} %cot_ref.1, bf16[12,128,128]{2,1,0:T(8,128)(2,1)} %raw_mix_ref.3, ...), custom_call_target="tpu_custom_call" | custom-call | tf_op jit(solution)/shard_map/pallas_call | solution.py:370
  67.1 0.0 copy-done
  67.1 0.0 copy-done.2
  67.1 0.0 copy-start.1
  67.1 0.9 %copy-done.1 = f32[16,16,128]{2,1,0:T(8,128)S(1)} copy-done((f32[16,16,128]{2,1,0:T(8,128)S(1)}, f32[16,16,128]{2,1,0:T(8,128)}, u32[]{:S(2)}) %copy-start.1) | copy-done | bytes 131096
  68.0 0.0 copy-start.5
  68.0 0.0 copy-start.3
  68.0 0.0 copy-start.4
  68.0 9.4 %shard_map.85 = bf16[128,256,128]{2,1,0:T(8,128)(2,1)} custom-call(bf16[4,128,64,128]{3,2,1,0:T(8,128)(2,1)} %get-tuple-element.9.back_ref, f32[256,128]{1,0:T(8,128)S(1)} %bitcast.4, bf16[12,128,128]{2,1,0:T(8,128)(2,1)S(1)} %copy-done, bf16[128,128]{1,0:T(8,128)(2,1)S(1)} %copy-done.2), custom_call_target="tpu_custom_call" | custom-call | flops 1073741824 | bytes 16777216 | tf_op jit(solution)/shard_map/pallas_call | solution.py:445
  77.4 0.0 copy-done.5
  77.4 0.5 slice_bitcast_fusion
  77.9 0.0 copy-done.3
  77.9 0.7 copy.11
  78.7 0.0 copy-done.4
  78.7 0.6 copy.12
  (1 shorter events, 0.0 us)
Async XLA Ops:
  0.6 66.4 %copy-start = (bf16[12,128,128]{2,1,0:T(8,128)(2,1)S(1)}, bf16[12,128,128]{2,1,0:T(8,128)(2,1)}, u32[]{:S(2)}) copy-start(bf16[12,128,128]{2,1,0:T(8,128)(2,1)} %raw_mix_ref.3) | copy-start | bytes 1179652
  0.6 66.4 %copy-start.2 = (bf16[128,128]{1,0:T(8,128)(2,1)S(1)}, bf16[128,128]{1,0:T(8,128)(2,1)}, u32[]{:S(2)}) copy-start(bf16[128,128]{1,0:T(8,128)(2,1)} %raw_point_ref.3) | copy-start | bytes 98308
  67.1 0.9 %copy-start.1 = (f32[16,16,128]{2,1,0:T(8,128)S(1)}, f32[16,16,128]{2,1,0:T(8,128)}, u32[]{:S(2)}) copy-start(f32[16,16,128]{2,1,0:T(8,128)} %get-tuple-element.10) | copy-start | bytes 393220
  68.0 9.4 %copy-start.5 = (f32[8,128]{1,0:T(8,128)S(1)}, f32[8,128]{1,0:T(8,128)}, u32[]{:S(2)}) copy-start(f32[8,128]{1,0:T(8,128)} %get-tuple-element.13) | copy-start | bytes 12292
  68.0 9.9 %copy-start.3 = (bf16[12,128,128]{2,1,0:T(8,128)(2,1)S(1)}, bf16[12,128,128]{2,1,0:T(8,128)(2,1)}, u32[]{:S(2)}) copy-start(bf16[12,128,128]{2,1,0:T(8,128)(2,1)} %get-tuple-element.19) | copy-start | bytes 1179652
  68.0 10.7 %copy-start.4 = (bf16[128,128]{1,0:T(8,128)(2,1)S(1)}, bf16[128,128]{1,0:T(8,128)(2,1)}, u32[]{:S(2)}) copy-start(bf16[128,128]{1,0:T(8,128)(2,1)} %get-tuple-element.20) | copy-start | bytes 98308
